TPU v7x, 512 devices: a whole 4x8x8 slice. The times are simulated.
512 devices in a mesh: row: 16 (over y, x_hi), col: 32 (over z, x_lo, core).
Axes of the slice: x: 4 (x_hi: 2, x_lo: 2; x = x_hi * 2 + x_lo), y: 8, z: 8, core: 2. Of those that a mesh axis runs over, the one named last changes fastest.
Arguments:
- sigma_anc: bfloat16 [4096, 4096], P('row', 'col'), as said below
- structure: int32 [512, 4], P(('row', 'col')), may hold values from 0 to 15, all different within a row
- factor: bfloat16 [512, 1024, 1024], P(('row', 'col')), may hold values from -0.375 to 0.375
- diag_term: float32 [512, 1024], P(('row', 'col')), may hold values from 1 to 8
Outputs:
- sigma_off: bfloat16 [512, 1024, 1024], P(('row', 'col'))
- variances: float32 [512, 1024], P(('row', 'col'))
Inputs may be any that keep to these rules, and one draw needn't show every extreme that they name: `structure`: each row names 4 different ancestor blocks, and every ancestor block is named by some row. sigma_anc is exactly symmetric, as the inverse of a symmetric precision matrix: its entry (p, q) equals its entry (q, p) bit for bit.
All inputs are finite; a program needn't handle non-finite values.
Results may differ from a plain program's by a relative error of at most 0.001.
Values may be sent and summed in bfloat16 or wider, within the bound.
No kernel may reach another device: no remote copies, remote signals or barrier semaphores. Data moves between devices by JAX's collectives and lax.ppermute only.
A program may use at most 64 MiB of HBM per device.

v0:
```python
import jax
import jax.numpy as jnp
from jax import lax
from jax.sharding import PartitionSpec as P


def body(sigma_anc, structure, factor, diag_term):
    span_count = structure.shape[1]
    block_rows = factor.shape[1] // span_count
    own_blocks = structure[0]
    triangle = factor[0]
    panel = lax.all_gather(sigma_anc, "col", axis=1, tiled=True)
    structures = lax.all_gather(structure, "row", axis=0, tiled=True)
    block_total = panel.shape[1] // block_rows
    blocked = panel.reshape(block_rows, block_total, block_rows)
    outgoing = jnp.take(blocked, structures, axis=1)
    outgoing = outgoing.reshape(block_rows, structures.shape[0], span_count * block_rows)
    received = lax.all_to_all(outgoing, "row", split_axis=1, concat_axis=1, tiled=True)
    picked = jnp.take(received, own_blocks, axis=1)
    product = jnp.einsum("bim,mw->ibw", picked, triangle, preferred_element_type=jnp.float32)
    off_block = -product.reshape(span_count * block_rows, triangle.shape[1])
    variance = diag_term[0] - jnp.sum(triangle.astype(jnp.float32) * off_block, axis=0)
    return (off_block.astype(jnp.bfloat16)[None], variance[None])


def solution(mesh):
    return jax.shard_map(
        body,
        mesh=mesh,
        in_specs=(
            P("row", "col"),
            P(("row", "col"), None),
            P(("row", "col"), None, None),
            P(("row", "col"), None),
        ),
        out_specs=(P(("row", "col"), None, None), P(("row", "col"), None)),
        check_vma=False,
    )
```

profile of v0, /device:TPU:1, one launch (start us, length us, event | category | flops | bytes accessed | tf_op | source)
XLA Modules:
  0.0 326.8 jit_solution(7711862939301773111)
XLA Ops:
  7.2 0.0 all-gather.3.cloned.1.call-start
  7.2 1.6 copy.21
  8.8 0.0 all-gather.3.cloned.1.call-update
  8.8 35.2 %all-gather = s32[16,1,4]{2,1,0:T(1,128)S(1)} all-gather(s32[1,1,4]{2,1,0:T(1,128)} %bitcast.47), channel_id=1, replica_groups=mesh['row'=16,'col'=32] {'row'}, dimensions={0}, use_global_device_ids=true | all-gather | bytes 272 | tf_op jit(solution)/shard_map/all_gather | solution.py:13
  44.0 0.1 copy.19
  44.1 0.1 copy.22
  44.2 0.1 reshape.70
  44.3 0.1 copy.20
  44.4 0.1 broadcast_in_dim.29
  44.5 39.6 %all-gather.3.cloned.1.call-done = bf16[256,4096]{0,1:T(8,128)(2,1)} async-done(((bf16[256,128]{0,1:T(8,128)(2,1)}), bf16[256,4096]{0,1:T(8,128)(2,1)}) %all-gather.3.cloned.1.call-update) | async-done | bytes 2097168 | tf_op jit(solution)/shard_map/all_gather | solution.py:12
  84.1 2.8 copy.23
  87.0 5.5 %gather_fusion = bf16[64,256,256]{2,1,0:T(8,128)(2,1)} fusion(bf16[256,16,256]{2,0,1:T(8,128)(2,1)S(1)} %copy.23, s32[1024]{0:T(1024)S(1)} %pad_clamp_fusion.1), kind=kCustom, calls=%fused_computation | custom fusion | bytes 16777472 | tf_op jit(solution)/shard_map/jit(_take)/gather | solution.py:16
  92.5 7.7 %copy.25 = bf16[16,4,32,8,256]{4,3,1,2,0:T(8,128)(2,1)} copy(bf16[16,4,32,8,256]{4,3,2,1,0:T(8,128)(2,1)} %bitcast.42) | data formatting | bytes 16777216 | tf_op jit(solution)/shard_map/jit(_take)/gather | solution.py:16
  100.2 7.4 %broadcast_select_fusion = bf16[256,16,1024]{2,0,1:T(8,128)(2,1)} fusion(bf16[256,16,1024]{2,0,1:T(8,128)(2,1)} %bitcast.41, pred[16,1024]{1,0:T(8,128)(4,1)S(1)} %bitcast.44), kind=kLoop, calls=%fused_computation.2 | loop fusion | flops 4194304 | bytes 16793600 | tf_op jit(solution)/shard_map/jit(_take)/select_n | solution.py:16
  107.6 0.0 copy-start.2
  107.6 8.9 %all-to-all-start = ((bf16[256,16,1024]{2,0,1:T(8,128)(2,1)}), bf16[256,16,1024]{2,0,1:T(8,128)(2,1)}, u32[]{:S(2)}, u32[]{:S(2)}) async-start(bf16[256,16,1024]{2,0,1:T(8,128)(2,1)} %broadcast_select_fusion), calls=%async_computation | async-start | bytes 16777216 | tf_op jit(solution)/shard_map/all_to_all | solution.py:18
  116.5 0.0 copy-done.2
  116.5 192.6 %all-to-all-done = bf16[256,16,1024]{2,0,1:T(8,128)(2,1)} async-done(((bf16[256,16,1024]{2,0,1:T(8,128)(2,1)}), bf16[256,16,1024]{2,0,1:T(8,128)(2,1)}, u32[]{:S(2)}, u32[]{:S(2)}) %all-to-all-start) | async-done | bytes 8388640 | tf_op jit(solution)/shard_map/all_to_all | solution.py:18
  309.1 4.1 %gather_fusion.1 = bf16[4,256,1024]{2,1,0:T(8,128)(2,1)S(1)} fusion(bf16[256,16,1024]{2,0,1:T(8,128)(2,1)} %all-to-all-done, s32[1024]{0:T(1024)S(1)} %pad_clamp_fusion), kind=kCustom, calls=%fused_computation.1 | custom fusion | bytes 4194320 | tf_op jit(solution)/shard_map/jit(_take)/gather | solution.py:19
  313.2 0.0 copy-start
  313.2 5.4 %fusion.8 = (bf16[256,4,1024]{2,0,1:T(8,128)(2,1)}, f32[256,4,1024]{2,0,1:T(8,128)S(1)}) fusion(bf16[1,1024,1024]{2,1,0:T(8,128)(2,1)} %param.6, bf16[4,256,1024]{2,1,0:T(8,128)(2,1)S(1)} %gather_fusion.1, pred[4]{0:T(512)(128)(4,1)S(1)} %compare_and_fusion.1), kind=kOutput, calls=%fused_computation.20 | convolution fusion | flops 2150629376 | bytes 10485764 | tf_op jit(solution)/shard_map/bim,mw->ibw/dot_general | solution.py:20
  318.7 0.0 copy-done
  318.7 0.0 copy-start.1
  318.7 0.5 fusion
  319.2 0.1 copy-done.1
  319.3 0.6 sub.4
  (7 shorter events, 0.0 us)
Async XLA Ops:
  7.2 77.0 %all-gather.3.cloned.1.call-start = ((), (), s32[]{:S(2)}) async-start(), calls=%async_computation.1 | async-start | bytes 2162688 | tf_op jit(solution)/shard_map/all_gather | solution.py:12
  107.6 8.9 %copy-start.2 = (s32[1,4]{1,0:T(1,128)S(1)}, s32[1,4]{1,0:T(1,128)}, u32[]{:S(2)}) copy-start(s32[1,4]{1,0:T(1,128)} %param.5) | copy-start | bytes 52
  107.6 201.6 %all-to-all-start = ((bf16[256,16,1024]{2,0,1:T(8,128)(2,1)}), bf16[256,16,1024]{2,0,1:T(8,128)(2,1)}, u32[]{:S(2)}, u32[]{:S(2)}) async-start(bf16[256,16,1024]{2,0,1:T(8,128)(2,1)} %broadcast_select_fusion), calls=%async_computation | async-start | bytes 16777216 | tf_op jit(solution)/shard_map/all_to_all | solution.py:18
  313.2 5.4 %copy-start = (bf16[1,1024,1024]{2,1,0:T(8,128)(2,1)S(1)}, bf16[1,1024,1024]{2,1,0:T(8,128)(2,1)}, u32[]{:S(2)}) copy-start(bf16[1,1024,1024]{2,1,0:T(8,128)(2,1)} %param.6) | copy-start | bytes 6291460
  318.7 0.7 copy-start.1
Sparse Core Ops, SparseCore 0:
  10.7 73.3 all-gather.2
where the time goes:
time: 329 us; the launch traced here: 327 us
  waiting for transfers between devices  232 us (71%)
  blocking collectives  35.2 us (11%)
  local copies, waits for them, and re-layouts  22.3 us (7%)
  between operations  14.1 us (4%)
  starting transfers between devices  8.9 us (3%)
  other arithmetic  8.57 us (3%)
  matrix products  5.43 us (2%)
    all_to_all x1, waiting for transfers between devices, body(): lax.all_to_all(outgoing, 'row', split_axis=1, concat_axis=1, tiled=True)  193 us
    all_gather x1, waiting for transfers between devices, body(): panel = lax.all_gather(sigma_anc, 'col', axis=1, tiled=True)  39.6 us
    all_gather x1, blocking collectives, body(): structures = lax.all_gather(structure, 'row', axis=0, tiled=True)  35.2 us
    gather x2, local copies, waits for them, and re-layouts, body(): outgoing = jnp.take(blocked, structures, axis=1)  13.2 us
    all_to_all x1, starting transfers between devices, body(): lax.all_to_all(outgoing, 'row', split_axis=1, concat_axis=1, tiled=True)  8.87 us
    select_n x2, other arithmetic, body(): outgoing = jnp.take(blocked, structures, axis=1)  7.4 us
  transfers between devices with their start and end apart: 2, of which 2 were waited for; matrix products, arithmetic and copies ran while one was open for 0% of the time, Pallas kernels for 0%

commit v1 on v0

v1 whole, which is shorter than its diff:
```python
import functools

import jax
import jax.numpy as jnp
from jax import lax
from jax.experimental import pallas as pl
from jax.experimental.pallas import tpu as pltpu
from jax.sharding import Mesh, PartitionSpec as P

Y, XH, Z, XL, C = 8, 2, 8, 2, 2
AXES = ("y", "xh", "z", "xl", "c")
CHIPS = ("y", "xh", "z", "xl")
PLANE = ("y", "z")
NB = 16
NU = Y * Z
S = 4
PAIRS = [(k, l) for k in range(S) for l in range(k, S)]


def rows_below(n, shape):
    return lax.broadcasted_iota(jnp.int32, shape, len(shape) - 2) < n


def deal_kernel(structure, sigma, out):
    lane = lax.broadcasted_iota(jnp.int32, (8, 128), 1)
    names = jnp.zeros((8, 128), jnp.float32)
    for k in range(S):
        names = jnp.where(lane == k, structure[0, k].astype(jnp.float32), names)
    top = rows_below(4, (8, 128))
    for u in range(NU):
        tile = sigma[pl.ds(8 * (u // 2), 8), :].astype(jnp.float32)
        if u % 2:
            tile = pltpu.roll(tile, 4, 0)
        tile = jnp.where(top, tile, names).astype(jnp.bfloat16)
        y, z = divmod(u, Z)
        for xh in range(XH):
            for xl in range(XL):
                out[((y * XH + xh) * Z + z) * XL + xl] = tile


def pick_kernel(place, names, own, other, out, slices):
    xh, xl, core = place[0], place[1], place[2]

    def merge(i, carry):
        at = pl.ds(pl.multiple_of(i * 8, 8), 8)
        mine = own[at].astype(jnp.float32)
        theirs = other[at].astype(jnp.float32)
        left = jnp.where(core == 0, mine, theirs)
        right = jnp.where(core == 0, theirs, mine)
        both = jnp.where(rows_below(4, left.shape), left, pltpu.roll(right, 4, 1))
        slices[at] = both.astype(jnp.bfloat16)
        return carry

    lax.fori_loop(0, NB * NB // 8, merge, 0)

    def pick(t, carry):
        y, z = t // Z, t % Z
        at = (((y * XH + xh) * Z + z) * XL + xl) * S
        name = [names[at + k] for k in range(S)]
        for p, (k, l) in enumerate(PAIRS):
            out[t, pl.ds(8 * p, 8), :] = slices[name[k] * NB + name[l]]
        return carry

    lax.fori_loop(0, NU, pick, 0)


def product_kernel(picked, factor, diag, off, variance, gram):
    @pl.when(pl.program_id(0) == 0)
    def _():
        for p, (k, l) in enumerate(PAIRS):
            part = picked[:, pl.ds(8 * p, 8), :].astype(jnp.float32)
            turned = pltpu.roll(part, 4, 1)
            part = part.reshape(NU // 2, 2, 8, 128)
            turned = turned.reshape(NU // 2, 2, 8, 128)
            top = rows_below(4, (NU // 2, 8, 128))
            halves = (
                jnp.where(top, part[:, 0], turned[:, 1]),
                jnp.where(top, turned[:, 0], part[:, 1]),
            )
            for h, half in enumerate(halves):
                half = half.reshape(256, 128).astype(jnp.bfloat16)
                gram[pl.ds(256 * k, 256), pl.ds(256 * l + 128 * h, 128)] = half
                if l > k:
                    gram[pl.ds(256 * l + 128 * h, 128), pl.ds(256 * k, 256)] = half.T

    minus = jnp.dot(gram[...], factor[0], preferred_element_type=jnp.float32)
    off[0] = (-minus).astype(jnp.bfloat16)
    total = jnp.sum(factor[0].astype(jnp.float32) * minus, axis=0, keepdims=True)
    variance[...] = diag[...] + total


def body(sigma, structure, factor, diag):
    width = factor.shape[2]
    tile = 256
    vmem, smem = pltpu.VMEM, pltpu.SMEM
    whole = pl.BlockSpec(memory_space=vmem)
    scalars = pl.BlockSpec(memory_space=smem)

    dealt = pl.pallas_call(
        deal_kernel,
        out_shape=jax.ShapeDtypeStruct((NB * NB, 8, 128), jnp.bfloat16),
        in_specs=[scalars, whole],
        out_specs=whole,
        name="deal",
    )(structure, sigma)
    own = lax.all_to_all(dealt, CHIPS, 0, 0, tiled=True)
    flip = [(d, d ^ 1) for d in range(2 * NB * NB)]
    other = lax.ppermute(own, AXES, flip)
    names = own[:, 4, :S].astype(jnp.int32).reshape(NB * NB * S)
    place = jnp.stack([lax.axis_index(a) for a in ("xh", "xl", "c")]).astype(jnp.int32)
    chosen = pl.pallas_call(
        pick_kernel,
        out_shape=jax.ShapeDtypeStruct((NU, 8 * len(PAIRS), 128), jnp.bfloat16),
        in_specs=[scalars, scalars, whole, whole],
        out_specs=whole,
        scratch_shapes=[vmem((NB * NB, 8, 128), jnp.bfloat16)],
        name="pick",
    )(place, names, own, other)
    picked = lax.all_to_all(chosen, PLANE, 0, 0, tiled=True)

    off, variance = pl.pallas_call(
        product_kernel,
        grid=(width // tile,),
        out_shape=(
            jax.ShapeDtypeStruct(factor.shape, jnp.bfloat16),
            jax.ShapeDtypeStruct(diag.shape, jnp.float32),
        ),
        in_specs=[
            whole,
            pl.BlockSpec((1, 1024, tile), lambda w: (0, 0, w)),
            pl.BlockSpec((1, tile), lambda w: (0, w)),
        ],
        out_specs=(
            pl.BlockSpec((1, 1024, tile), lambda w: (0, 0, w)),
            pl.BlockSpec((1, tile), lambda w: (0, w)),
        ),
        scratch_shapes=[vmem((1024, 1024), jnp.bfloat16)],
        name="product",
    )(picked, factor, diag)
    return off, variance


def solution(mesh):
    fine = Mesh(mesh.devices.reshape(Y, XH, Z, XL, C), AXES)
    return jax.shard_map(
        body,
        mesh=fine,
        in_specs=(
            P(("y", "xh"), ("z", "xl", "c")),
            P(AXES, None),
            P(AXES, None, None),
            P(AXES, None),
        ),
        out_specs=(P(AXES, None, None), P(AXES, None)),
        check_vma=False,
    )
```

time: 329 us -> 103 us (0.31)
  waiting for transfers between devices: 232 us -> 0.01 us
  blocking collectives: 35.2 us -> 80.9 us
  local copies, waits for them, and re-layouts: 22.3 us -> 1.52 us
  between operations: 14.1 us -> 0.65 us
  Pallas kernels: 0 us -> 12.5 us
  other arithmetic: 8.57 us -> 1.07 us
  matrix products: 5.43 us -> 0 us
  starting transfers between devices: 8.9 us -> 4.25 us
    all_to_all x1 -> x0, waiting for transfers between devices: 193 us -> none  [body(): lax.all_to_all(outgoing, 'row', split_axis=1, concat_axis=1, tiled=True)]
    all_to_all x0 -> x2, blocking collectives: none -> 80.9 us  [the longest x1 42 us: body(): own = lax.all_to_all(dealt, CHIPS, 0, 0, tiled=True)]
    all_gather x1 -> x0, waiting for transfers between devices: 39.6 us -> none  [body(): panel = lax.all_gather(sigma_anc, 'col', axis=1, tiled=True)]
    all_gather x1 -> x0, blocking collectives: 35.2 us -> none  [body(): structures = lax.all_gather(structure, 'row', axis=0, tiled=True)]
    gather x3 -> x0, local copies, waits for them, and re-layouts: 17.3 us -> none  [the longest x2 13.2 us: body(): outgoing = jnp.take(blocked, structures, axis=1)]
    pallas_call x0 -> x3, Pallas kernels: none -> 12.5 us  [the longest x1 6.51 us: body(): pl.pallas_call(product_kernel, grid=(width // tile,), out_shape=(jax.Shap...]
    all_to_all x1 -> x0, starting transfers between devices: 8.87 us -> none  [body(): lax.all_to_all(outgoing, 'row', split_axis=1, concat_axis=1, tiled=True)]
    select_n x3 -> x0, other arithmetic: 7.4 us -> none  [the longest x2 7.4 us: body(): outgoing = jnp.take(blocked, structures, axis=1)]
  transfers between devices with their start and end apart: 2 -> 1, of which waited for: 2 -> 0; matrix products, arithmetic and copies ran while one was open for 0% -> 2% of each run, Pallas kernels for 0% -> 0%
where the time goes in v1:
time: 103 us; the launch traced here: 101 us
  blocking collectives  80.9 us (79%)
  Pallas kernels  12.5 us (12%)
  starting transfers between devices  4.25 us (4%)
  local copies, waits for them, and re-layouts  1.52 us (1%)
  other arithmetic  1.07 us (1%)
    all_to_all x1, blocking collectives, body(): own = lax.all_to_all(dealt, CHIPS, 0, 0, tiled=True)  42 us
    all_to_all x1, blocking collectives, body(): picked = lax.all_to_all(chosen, PLANE, 0, 0, tiled=True)  39 us
    pallas_call x1, Pallas kernels, body(): pl.pallas_call(product_kernel, grid=(width // tile,), out_shape=(jax.Shap...  6.51 us
    pallas_call x1, Pallas kernels, body(): pl.pallas_call(pick_kernel, out_shape=jax.ShapeDtypeStruct((NU, 8 * len(P...  4.29 us
    ppermute x1, starting transfers between devices, body(): other = lax.ppermute(own, AXES, flip)  4.25 us
  transfers between devices with their start and end apart: 1, of which 0 were waited for; matrix products, arithmetic and copies ran while one was open for 2% of the time, Pallas kernels for 0%

profile of v1, /device:TPU:1, one launch (start us, length us, event | category | flops | bytes accessed | tf_op | source)
XLA Modules:
  0.0 100.9 jit_solution(981394247297415822)
XLA Ops:
  0.6 1.7 %deal.1 = bf16[256,8,128]{2,1,0:T(8,128)(2,1)} custom-call(s32[1,4]{1,0:T(1,128)} %structure.1, bf16[256,128]{1,0:T(8,128)(2,1)} %sigma.1), custom_call_target="tpu_custom_call" | custom-call | tf_op jit(solution)/shard_map/deal/pallas_call | solution.py:99
  2.3 42.0 %all_to_all.10.own = bf16[256,8,128]{2,1,0:T(8,128)(2,1)S(1)} all-to-all(bf16[256,8,128]{2,1,0:T(8,128)(2,1)} %deal.1), channel_id=1, replica_groups=mesh['y'=8,'xh'=2,'z'=8,'xl'=2,'c'=2] {'y','xh','z','xl'}, dimensions={0} | all-to-all | bytes 1048576 | tf_op jit(solution)/shard_map/all_to_all | solution.py:106
  44.3 0.0 copy-start
  44.3 4.2 %collective-permute-start = (bf16[256,8,128]{2,1,0:T(8,128)(2,1)S(1)}, bf16[256,8,128]{2,1,0:T(8,128)(2,1)S(1)}, u32[]{:S(2)}, u32[]{:S(2)}) collective-permute-start(bf16[256,8,128]{2,1,0:T(8,128)(2,1)S(1)} %all_to_all.10.own), channel_id=1, source_target_pairs={{0,1},{1,0},{2,3},{3,2},{4,5},{5,4},{6,7},{7,6},{8,9},{9,8},{10,11... | collective-permute-start | bytes 1572872 | tf_op jit(solution)/shard_map/ppermute | solution.py:108
  48.5 0.6 pad_add_fusion.place
  49.1 0.5 fusion
  49.6 0.7 reshape.8.names
  50.3 0.0 collective-permute-done.other
  50.3 0.0 copy-done
  50.3 0.0 copy-start.1
  50.3 0.8 copy-done.1
  51.1 4.3 %pick.1 = bf16[64,80,128]{2,1,0:T(8,128)(2,1)} custom-call(s32[3]{0:T(128)} %pad_add_fusion.place, s32[1024]{0:T(1024)} %reshape.8.names, bf16[256,8,128]{2,1,0:T(8,128)(2,1)} %copy-done, bf16[256,8,128]{2,1,0:T(8,128)(2,1)} %copy-done.1), custom_call_target="tpu_custom_call" | custom-call | tf_op jit(solution)/shard_map/pick/pallas_call | solution.py:111
  55.4 39.0 %all_to_all.11.picked = bf16[64,80,128]{2,1,0:T(8,128)(2,1)} all-to-all(bf16[64,80,128]{2,1,0:T(8,128)(2,1)} %pick.1), channel_id=1, replica_groups=mesh['y'=8,'xh'=2,'z'=8,'xl'=2,'c'=2] {'y','z'}, dimensions={0} | all-to-all | bytes 2621440 | tf_op jit(solution)/shard_map/all_to_all | solution.py:119
  94.4 6.5 %product.1 = (bf16[1,1024,1024]{2,1,0:T(8,128)(2,1)}, f32[1,1024]{1,0:T(1,128)}) custom-call(bf16[64,80,128]{2,1,0:T(8,128)(2,1)} %all_to_all.11.picked, bf16[1,1024,1024]{2,1,0:T(8,128)(2,1)} %factor.1, f32[1,1024]{1,0:T(1,128)} %diag.1), custom_call_target="tpu_custom_call" | custom-call | tf_op jit(solution)/shard_map/product/pallas_call | solution.py:121
Async XLA Ops:
  44.3 6.1 %copy-start = (bf16[256,8,128]{2,1,0:T(8,128)(2,1)}, bf16[256,8,128]{2,1,0:T(8,128)(2,1)S(1)}, u32[]{:S(2)}) copy-start(bf16[256,8,128]{2,1,0:T(8,128)(2,1)S(1)} %all_to_all.10.own) | copy-start | bytes 1572868
  44.3 6.0 %collective-permute-start = (bf16[256,8,128]{2,1,0:T(8,128)(2,1)S(1)}, bf16[256,8,128]{2,1,0:T(8,128)(2,1)S(1)}, u32[]{:S(2)}, u32[]{:S(2)}) collective-permute-start(bf16[256,8,128]{2,1,0:T(8,128)(2,1)S(1)} %all_to_all.10.own), channel_id=1, source_target_pairs={{0,1},{1,0},{2,3},{3,2},{4,5},{5,4},{6,7},{7,6},{8,9},{9,8},{10,11... | collective-permute-start | bytes 1572872 | tf_op jit(solution)/shard_map/ppermute | solution.py:108
  50.3 0.8 copy-start.1

commit v2 on v1

v2 whole, which is shorter than its diff:
```python
import jax
import jax.numpy as jnp
from jax import lax
from jax.experimental import pallas as pl
from jax.experimental.pallas import tpu as pltpu
from jax.sharding import Mesh, PartitionSpec as P

Y, XH, Z, XL, C = 8, 2, 8, 2, 2
AXES = ("y", "xh", "z", "xl", "c")
CHIPS = ("y", "xh", "z", "xl")
PLANE = ("y", "z")
NB = 16
NU = Y * Z
S = 4
PAIRS = [(k, l) for k in range(S) for l in range(k, S)]


def rows_below(n, shape):
    return lax.broadcasted_iota(jnp.int32, shape, len(shape) - 2) < n


def deal_kernel(structure, sigma, out):
    lane = lax.broadcasted_iota(jnp.int32, (8, 128), 1)
    names = jnp.zeros((8, 128), jnp.float32)
    for k in range(S):
        names = jnp.where(lane == k, structure[0, k].astype(jnp.float32), names)
    top = rows_below(4, (8, 128))
    for u in range(NU):
        tile = sigma[pl.ds(8 * (u // 2), 8), :].astype(jnp.float32)
        if u % 2:
            tile = pltpu.roll(tile, 4, 0)
        tile = jnp.where(top, tile, names).astype(jnp.bfloat16)
        y, z = divmod(u, Z)
        for xh in range(XH):
            for xl in range(XL):
                out[((y * XH + xh) * Z + z) * XL + xl] = tile


def pick_kernel(names, own, other, out, slices):
    xh, xl, core = (lax.axis_index(a) for a in ("xh", "xl", "c"))

    def merge(left, right):
        def step(i, carry):
            at = pl.ds(pl.multiple_of(i * 32, 32), 32)
            low = pltpu.roll(right[at].astype(jnp.float32), 4, 1)
            both = jnp.where(rows_below(4, low.shape), left[at].astype(jnp.float32), low)
            slices[at] = both.astype(jnp.bfloat16)
            return carry

        lax.fori_loop(0, NB * NB // 32, step, 0)

    @pl.when(core == 0)
    def _():
        merge(own, other)

    @pl.when(core != 0)
    def _():
        merge(other, own)

    def pick(y, carry):
        first = ((y * XH + xh) * Z * XL + xl) * S
        for z in range(Z):
            name = [names[first + z * XL * S + k] for k in range(S)]
            high = [n * NB for n in name]
            for p, (k, l) in enumerate(PAIRS):
                out[y * Z + z, pl.ds(8 * p, 8), :] = slices[high[k] + name[l]]
        return carry

    lax.fori_loop(0, Y, pick, 0)


def unfold(picked, p):
    part = picked[:, pl.ds(8 * p, 8), :].astype(jnp.float32)
    turned = pltpu.roll(part, 4, 1)
    part = part.reshape(NU // 2, 2, 8, 128)
    turned = turned.reshape(NU // 2, 2, 8, 128)
    top = rows_below(4, (NU // 2, 8, 128))
    left = jnp.where(top, part[:, 0], turned[:, 1])
    right = jnp.where(top, turned[:, 0], part[:, 1])
    return [h.reshape(256, 128).astype(jnp.bfloat16) for h in (left, right)]


def product_kernel(picked, factor, diag, off, variance, gram, staged, sems):
    total = diag[...]
    copies = []
    for k in range(S):
        rows = pl.ds(256 * k, 256)
        for l in range(k, S):
            for h, half in enumerate(unfold(picked, PAIRS.index((k, l)))):
                columns = pl.ds(256 * l + 128 * h, 128)
                gram[rows, columns] = half
                if l > k:
                    gram[columns, rows] = half.T
        minus = jnp.dot(gram[rows, :], factor[0], preferred_element_type=jnp.float32)
        staged[k] = (-minus).astype(jnp.bfloat16)
        copies.append(pltpu.make_async_copy(staged.at[k], off.at[0, rows], sems.at[k]))
        copies[k].start()
        total += jnp.sum(
            factor[0, rows, :].astype(jnp.float32) * minus, axis=0, keepdims=True
        )
    variance[...] = total
    for copy in copies:
        copy.wait()


def body(sigma, structure, factor, diag):
    vmem, smem = pltpu.VMEM, pltpu.SMEM
    whole = pl.BlockSpec(memory_space=vmem)
    scalars = pl.BlockSpec(memory_space=smem)

    dealt = pl.pallas_call(
        deal_kernel,
        out_shape=jax.ShapeDtypeStruct((NB * NB, 8, 128), jnp.bfloat16),
        in_specs=[scalars, whole],
        out_specs=whole,
        compiler_params=pltpu.CompilerParams(vmem_limit_bytes=2 << 20),
        name="deal",
    )(structure, sigma)
    own = lax.all_to_all(dealt, CHIPS, 0, 0, tiled=True)
    flip = [(d, d ^ 1) for d in range(2 * NB * NB)]
    other = lax.ppermute(own, AXES, flip)
    names = own[:, 4, :S].astype(jnp.int32).reshape(NB * NB * S)
    chosen = pl.pallas_call(
        pick_kernel,
        out_shape=jax.ShapeDtypeStruct((NU, 8 * len(PAIRS), 128), jnp.bfloat16),
        in_specs=[scalars, whole, whole],
        out_specs=whole,
        scratch_shapes=[vmem((NB * NB, 8, 128), jnp.bfloat16)],
        compiler_params=pltpu.CompilerParams(vmem_limit_bytes=6 << 20),
        name="pick",
    )(names, own, other)
    picked = lax.all_to_all(chosen, PLANE, 0, 0, tiled=True)

    off, variance = pl.pallas_call(
        product_kernel,
        out_shape=(
            jax.ShapeDtypeStruct(factor.shape, jnp.bfloat16),
            jax.ShapeDtypeStruct(diag.shape, jnp.float32),
        ),
        in_specs=[whole, whole, whole],
        out_specs=(pl.BlockSpec(memory_space=pl.ANY), whole),
        scratch_shapes=[
            vmem((1024, 1024), jnp.bfloat16),
            vmem((S, 256, 1024), jnp.bfloat16),
            pltpu.SemaphoreType.DMA((S,)),
        ],
        compiler_params=pltpu.CompilerParams(vmem_limit_bytes=24 << 20),
        name="product",
    )(picked, factor, diag)
    return off, variance


def solution(mesh):
    fine = Mesh(mesh.devices.reshape(Y, XH, Z, XL, C), AXES)
    return jax.shard_map(
        body,
        mesh=fine,
        in_specs=(
            P(("y", "xh"), ("z", "xl", "c")),
            P(AXES, None),
            P(AXES, None, None),
            P(AXES, None),
        ),
        out_specs=(P(AXES, None, None), P(AXES, None)),
        check_vma=False,
    )
```

time: 103 us -> 95.5 us (0.927)
  the two profiles are of different devices: /device:TPU:1 before, /device:TPU:16 now
where the time goes in v2:
time: 95.5 us; the launch traced here: 95.2 us
  blocking collectives  83.2 us (87%)
  Pallas kernels  6.09 us (6%)
  starting transfers between devices  1.91 us (2%)
  local copies, waits for them, and re-layouts  1.62 us (2%)
  waiting for transfers between devices  1.25 us (1%)
    all_to_all x1, blocking collectives, body(): own = lax.all_to_all(dealt, CHIPS, 0, 0, tiled=True)  41.7 us
    all_to_all x1, blocking collectives, body(): picked = lax.all_to_all(chosen, PLANE, 0, 0, tiled=True)  41.5 us
    pallas_call x1, Pallas kernels, body(): pl.pallas_call(product_kernel, out_shape=(jax.ShapeDtypeStruct(factor.sha...  3.95 us
  transfers between devices with their start and end apart: 1, of which 1 were waited for; matrix products, arithmetic and copies ran while one was open for 1% of the time, Pallas kernels for 0%

profile of v2, /device:TPU:16, one launch (start us, length us, event | category | flops | bytes accessed | tf_op | source)
XLA Modules:
  0.0 95.2 jit_solution(9796874630133606361)
XLA Ops:
  0.6 0.0 copy-start.1
  0.6 0.8 copy-done.1
  1.5 0.0 copy-start.3
  1.5 0.7 copy-done.3
  2.1 0.6 deal.1
  2.7 41.7 %all_to_all.10.own = bf16[256,8,128]{2,1,0:T(8,128)(2,1)S(1)} all-to-all(bf16[256,8,128]{2,1,0:T(8,128)(2,1)S(1)} %deal.1), channel_id=1, replica_groups=mesh['y'=8,'xh'=2,'z'=8,'xl'=2,'c'=2] {'y','xh','z','xl'}, dimensions={0} | all-to-all | bytes 1048576 | tf_op jit(solution)/shard_map/all_to_all | solution.py:119
  44.4 1.9 %collective-permute-start = (bf16[256,8,128]{2,1,0:T(8,128)(2,1)S(1)}, bf16[256,8,128]{2,1,0:T(8,128)(2,1)S(1)}, u32[]{:S(2)}, u32[]{:S(2)}) collective-permute-start(bf16[256,8,128]{2,1,0:T(8,128)(2,1)S(1)} %all_to_all.10.own), channel_id=1, source_target_pairs={{0,1},{1,0},{2,3},{3,2},{4,5},{5,4},{6,7},{7,6},{8,9},{9,8},{10,11... | collective-permute-start | bytes 1572872 | tf_op jit(solution)/shard_map/ppermute | solution.py:121
  46.4 0.5 fusion
  46.8 0.1 reshape.8.names
  47.0 0.0 copy-start
  47.0 0.0 copy-start.2
  47.0 1.2 %collective-permute-done.other = bf16[256,8,128]{2,1,0:T(8,128)(2,1)S(1)} collective-permute-done((bf16[256,8,128]{2,1,0:T(8,128)(2,1)S(1)}, bf16[256,8,128]{2,1,0:T(8,128)(2,1)S(1)}, u32[]{:S(2)}, u32[]{:S(2)}) %collective-permute-start) | collective-permute-done | bytes 524320 | tf_op jit(solution)/shard_map/ppermute | solution.py:121
  48.2 1.6 %pick.1 = bf16[64,80,128]{2,1,0:T(8,128)(2,1)S(1)} custom-call(s32[1024]{0:T(1024)S(1)} %reshape.8.names, bf16[256,8,128]{2,1,0:T(8,128)(2,1)S(1)} %all_to_all.10.own, bf16[256,8,128]{2,1,0:T(8,128)(2,1)S(1)} %collective-permute-done.other), custom_call_target="tpu_custom_call" | custom-call | tf_op jit(solution)/shard_map/pick/pallas_call | solution.py:123
  49.8 41.5 %all_to_all.11.picked = bf16[64,80,128]{2,1,0:T(8,128)(2,1)S(1)} all-to-all(bf16[64,80,128]{2,1,0:T(8,128)(2,1)S(1)} %pick.1), channel_id=1, replica_groups=mesh['y'=8,'xh'=2,'z'=8,'xl'=2,'c'=2] {'y','z'}, dimensions={0} | all-to-all | bytes 2621440 | tf_op jit(solution)/shard_map/all_to_all | solution.py:132
  91.3 0.0 copy-done
  91.3 0.0 copy-done.2
  91.3 3.9 %product.1 = (bf16[1,1024,1024]{2,1,0:T(8,128)(2,1)}, f32[1,1024]{1,0:T(1,128)}) custom-call(bf16[64,80,128]{2,1,0:T(8,128)(2,1)S(1)} %all_to_all.11.picked, bf16[1,1024,1024]{2,1,0:T(8,128)(2,1)S(1)} %copy-done, f32[1,1024]{1,0:T(1,128)S(1)} %copy-done.2), custom_call_target="tpu_custom_call" | custom-call | tf_op jit(solution)/shard_map/product/pallas_call | solution.py:134
Async XLA Ops:
  0.6 0.8 copy-start.1
  1.5 0.7 copy-start.3
  44.4 3.8 %collective-permute-start = (bf16[256,8,128]{2,1,0:T(8,128)(2,1)S(1)}, bf16[256,8,128]{2,1,0:T(8,128)(2,1)S(1)}, u32[]{:S(2)}, u32[]{:S(2)}) collective-permute-start(bf16[256,8,128]{2,1,0:T(8,128)(2,1)S(1)} %all_to_all.10.own), channel_id=1, source_target_pairs={{0,1},{1,0},{2,3},{3,2},{4,5},{5,4},{6,7},{7,6},{8,9},{9,8},{10,11... | collective-permute-start | bytes 1572872 | tf_op jit(solution)/shard_map/ppermute | solution.py:121
  47.0 44.3 %copy-start = (bf16[1,1024,1024]{2,1,0:T(8,128)(2,1)S(1)}, bf16[1,1024,1024]{2,1,0:T(8,128)(2,1)}, u32[]{:S(2)}) copy-start(bf16[1,1024,1024]{2,1,0:T(8,128)(2,1)} %factor.1) | copy-start | bytes 6291460
  47.0 44.3 %copy-start.2 = (f32[1,1024]{1,0:T(1,128)S(1)}, f32[1,1024]{1,0:T(1,128)}, u32[]{:S(2)}) copy-start(f32[1,1024]{1,0:T(1,128)} %diag.1) | copy-start | bytes 12292

commit v3 on v2

--- a/solution.py
+++ b/solution.py
@@ -12,32 +12,56 @@
 NB = 16
 NU = Y * Z
 S = 4
-PAIRS = [(k, l) for k in range(S) for l in range(k, S)]
+PAIRS = [(k, l) for k in range(S) for l in range(k + 1, S)]
+ROWS = 8 * len(PAIRS) + 4 * S
 
 
 def rows_below(n, shape):
     return lax.broadcasted_iota(jnp.int32, shape, len(shape) - 2) < n
 
 
-def deal_kernel(structure, sigma, out):
+def deal_kernel(structure_hbm, sigma_hbm, dealt, structure, sigma, out, sems, out_sems):
+    copies = [
+        pltpu.make_async_copy(structure_hbm, structure, sems.at[0]),
+        pltpu.make_async_copy(sigma_hbm, sigma, sems.at[1]),
+    ]
+    for copy in copies:
+        copy.start()
+    for copy in copies:
+        copy.wait()
     lane = lax.broadcasted_iota(jnp.int32, (8, 128), 1)
-    names = jnp.zeros((8, 128), jnp.float32)
+    row = lax.broadcasted_iota(jnp.int32, (8, 128), 0)
+    extra = jnp.zeros((8, 128), jnp.float32)
     for k in range(S):
-        names = jnp.where(lane == k, structure[0, k].astype(jnp.float32), names)
-    top = rows_below(4, (8, 128))
+        extra = jnp.where(lane == k, structure[0, k].astype(jnp.float32), extra)
+    start = pl.multiple_of(128 * (1 - lax.axis_index("c")), 128)
+    square = sigma[pl.ds(start, 128), :].astype(jnp.float32)
+    on = lax.broadcasted_iota(jnp.int32, (128, 128), 0) == lax.broadcasted_iota(
+        jnp.int32, (128, 128), 1
+    )
+    far = jnp.sum(jnp.where(on, square, 0.0), axis=0, keepdims=True)
+    extra = jnp.where(row == 5, far, extra)
     for u in range(NU):
         tile = sigma[pl.ds(8 * (u // 2), 8), :].astype(jnp.float32)
         if u % 2:
             tile = pltpu.roll(tile, 4, 0)
-        tile = jnp.where(top, tile, names).astype(jnp.bfloat16)
+        tile = jnp.where(row < 4, tile, extra).astype(jnp.bfloat16)
         y, z = divmod(u, Z)
         for xh in range(XH):
             for xl in range(XL):
                 out[((y * XH + xh) * Z + z) * XL + xl] = tile
-
-
-def pick_kernel(names, own, other, out, slices):
-    xh, xl, core = (lax.axis_index(a) for a in ("xh", "xl", "c"))
+        if z == Z - 1:
+            part = pl.ds(y * XH * Z * XL, XH * Z * XL)
+            copies.append(
+                pltpu.make_async_copy(out.at[part], dealt.at[part], out_sems.at[y])
+            )
+            copies[-1].start()
+    for copy in copies[2:]:
+        copy.wait()
+
+
+def pick_kernel(names, own, other, out, far, slices, bands):
+    y_me, xh, z_me, xl, core = (lax.axis_index(a) for a in AXES)
 
     def merge(left, right):
         def step(i, carry):
@@ -48,6 +72,15 @@
             return carry
 
         lax.fori_loop(0, NB * NB // 32, step, 0)
+        lane = lax.broadcasted_iota(jnp.int32, (8, 128), 1)
+        i = 4 * (y_me * Z + z_me) + lax.broadcasted_iota(jnp.int32, (8, 128), 0)
+        near = ((lane - i) & 255) < 128
+        for r in range(NB):
+            at = r * (NB + 1)
+            band = jnp.where(
+                near, left[at].astype(jnp.float32), right[at].astype(jnp.float32)
+            )
+            bands[r] = band.astype(jnp.bfloat16)
 
     @pl.when(core == 0)
     def _():
@@ -57,13 +90,22 @@
     def _():
         merge(other, own)
 
+    mine = (((y_me * XH + xh) * Z + z_me) * XL + xl) * S
+    for k in range(S):
+        spare = own[names[mine + k] * (NB + 1), pl.ds(4, 4), :].astype(jnp.float32)
+        far[pl.ds(k, 1), :] = spare[1:2]
+
     def pick(y, carry):
         first = ((y * XH + xh) * Z * XL + xl) * S
         for z in range(Z):
+            t = y * Z + z
             name = [names[first + z * XL * S + k] for k in range(S)]
             high = [n * NB for n in name]
             for p, (k, l) in enumerate(PAIRS):
-                out[y * Z + z, pl.ds(8 * p, 8), :] = slices[high[k] + name[l]]
+                out[t, pl.ds(8 * p, 8), :] = slices[high[k] + name[l]]
+            for k in range(S):
+                rows = pl.ds(8 * len(PAIRS) + 4 * k, 4)
+                out[t, rows, :] = bands[name[k], pl.ds(0, 4), :]
         return carry
 
     lax.fori_loop(0, Y, pick, 0)
@@ -77,20 +119,40 @@
     top = rows_below(4, (NU // 2, 8, 128))
     left = jnp.where(top, part[:, 0], turned[:, 1])
     right = jnp.where(top, turned[:, 0], part[:, 1])
-    return [h.reshape(256, 128).astype(jnp.bfloat16) for h in (left, right)]
-
-
-def product_kernel(picked, factor, diag, off, variance, gram, staged, sems):
+    return [h.reshape(256, 128) for h in (left, right)]
+
+
+def square_of(band, far):
+    upper, lower = band[:128], band[128:]
+    row = lax.broadcasted_iota(jnp.int32, (128, 128), 0)
+    lane = lax.broadcasted_iota(jnp.int32, (128, 128), 1)
+    over, under = lane > row, lane < row
+    quarters = (
+        (jnp.where(under, upper.T, upper), jnp.where(under, upper, lower.T)),
+        (jnp.where(under, lower, upper.T), jnp.where(under, lower.T, lower)),
+    )
+    mixed = [jnp.where(over | under, quarters[h][1 - h], far) for h in range(2)]
+    return ((quarters[0][0], mixed[0]), (mixed[1], quarters[1][1]))
+
+
+def product_kernel(picked, far, factor, diag, off, variance, gram, staged, sems):
     total = diag[...]
     copies = []
     for k in range(S):
         rows = pl.ds(256 * k, 256)
-        for l in range(k, S):
+        if k % 2 == 0:
+            bands = unfold(picked, len(PAIRS) + k // 2)
+        quarters = square_of(bands[k % 2], far[pl.ds(k, 1), :])
+        for g in range(2):
+            for h in range(2):
+                at = (pl.ds(256 * k + 128 * g, 128), pl.ds(256 * k + 128 * h, 128))
+                gram[at] = quarters[g][h].astype(jnp.bfloat16)
+        for l in range(k + 1, S):
             for h, half in enumerate(unfold(picked, PAIRS.index((k, l)))):
                 columns = pl.ds(256 * l + 128 * h, 128)
+                half = half.astype(jnp.bfloat16)
                 gram[rows, columns] = half
-                if l > k:
-                    gram[columns, rows] = half.T
+                gram[columns, rows] = half.T
         minus = jnp.dot(gram[rows, :], factor[0], preferred_element_type=jnp.float32)
         staged[k] = (-minus).astype(jnp.bfloat16)
         copies.append(pltpu.make_async_copy(staged.at[k], off.at[0, rows], sems.at[k]))
@@ -107,25 +169,38 @@
     vmem, smem = pltpu.VMEM, pltpu.SMEM
     whole = pl.BlockSpec(memory_space=vmem)
     scalars = pl.BlockSpec(memory_space=smem)
+    anywhere = pl.BlockSpec(memory_space=pl.ANY)
 
     dealt = pl.pallas_call(
         deal_kernel,
         out_shape=jax.ShapeDtypeStruct((NB * NB, 8, 128), jnp.bfloat16),
-        in_specs=[scalars, whole],
-        out_specs=whole,
-        compiler_params=pltpu.CompilerParams(vmem_limit_bytes=2 << 20),
+        in_specs=[anywhere, anywhere],
+        out_specs=anywhere,
+        scratch_shapes=[
+            smem(structure.shape, jnp.int32),
+            vmem(sigma.shape, jnp.bfloat16),
+            vmem((NB * NB, 8, 128), jnp.bfloat16),
+            pltpu.SemaphoreType.DMA((2,)),
+            pltpu.SemaphoreType.DMA((Y,)),
+        ],
         name="deal",
     )(structure, sigma)
     own = lax.all_to_all(dealt, CHIPS, 0, 0, tiled=True)
     flip = [(d, d ^ 1) for d in range(2 * NB * NB)]
     other = lax.ppermute(own, AXES, flip)
     names = own[:, 4, :S].astype(jnp.int32).reshape(NB * NB * S)
-    chosen = pl.pallas_call(
+    chosen, far = pl.pallas_call(
         pick_kernel,
-        out_shape=jax.ShapeDtypeStruct((NU, 8 * len(PAIRS), 128), jnp.bfloat16),
+        out_shape=(
+            jax.ShapeDtypeStruct((NU, ROWS, 128), jnp.bfloat16),
+            jax.ShapeDtypeStruct((8, 128), jnp.float32),
+        ),
         in_specs=[scalars, whole, whole],
-        out_specs=whole,
-        scratch_shapes=[vmem((NB * NB, 8, 128), jnp.bfloat16)],
+        out_specs=(whole, whole),
+        scratch_shapes=[
+            vmem((NB * NB, 8, 128), jnp.bfloat16),
+            vmem((NB, 8, 128), jnp.bfloat16),
+        ],
         compiler_params=pltpu.CompilerParams(vmem_limit_bytes=6 << 20),
         name="pick",
     )(names, own, other)
@@ -137,8 +212,8 @@
             jax.ShapeDtypeStruct(factor.shape, jnp.bfloat16),
             jax.ShapeDtypeStruct(diag.shape, jnp.float32),
         ),
-        in_specs=[whole, whole, whole],
-        out_specs=(pl.BlockSpec(memory_space=pl.ANY), whole),
+        in_specs=[whole, whole, whole, whole],
+        out_specs=(anywhere, whole),
         scratch_shapes=[
             vmem((1024, 1024), jnp.bfloat16),
             vmem((S, 256, 1024), jnp.bfloat16),
@@ -146,7 +221,7 @@
         ],
         compiler_params=pltpu.CompilerParams(vmem_limit_bytes=24 << 20),
         name="product",
-    )(picked, factor, diag)
+    )(picked, far, factor, diag)
     return off, variance
 
 

time: 95.5 us -> 90.3 us (0.946)
  blocking collectives: 83.2 us -> 78.2 us
  local copies, waits for them, and re-layouts: 1.62 us -> 0.13 us
  Pallas kernels: 6.09 us -> 7.35 us
    all_to_all x1, blocking collectives: 41.5 us -> 36.1 us  [body(): picked = lax.all_to_all(chosen, PLANE, 0, 0, tiled=True)]
    unnamed x8 -> x4, local copies, waits for them, and re-layouts: 1.5 us -> 0.01 us
    pallas_call x1, Pallas kernels: 0.58 us -> 1.74 us  [body(): pl.pallas_call(deal_kernel, out_shape=jax.ShapeDtypeStruct((NB * NB, 8, 1...]
where the time goes in v3:
time: 90.3 us; the launch traced here: 90 us
  blocking collectives  78.2 us (87%)
  Pallas kernels  7.35 us (8%)
  starting transfers between devices  1.91 us (2%)
  waiting for transfers between devices  1.27 us (1%)
    all_to_all x1, blocking collectives, body(): own = lax.all_to_all(dealt, CHIPS, 0, 0, tiled=True)  42 us
    all_to_all x1, blocking collectives, body(): picked = lax.all_to_all(chosen, PLANE, 0, 0, tiled=True)  36.1 us
    pallas_call x1, Pallas kernels, body(): pl.pallas_call(product_kernel, out_shape=(jax.ShapeDtypeStruct(factor.sha...  4.11 us
    ppermute x1, starting transfers between devices, body(): other = lax.ppermute(own, AXES, flip)  1.91 us
  transfers between devices with their start and end apart: 1, of which 1 were waited for; matrix products, arithmetic and copies ran while one was open for 1% of the time, Pallas kernels for 0%

profile of v3, /device:TPU:16, one launch (start us, length us, event | category | flops | bytes accessed | tf_op | source)
XLA Modules:
  0.0 90.0 jit_solution(13555626252999627629)
XLA Ops:
  0.6 1.7 %deal.1 = bf16[256,8,128]{2,1,0:T(8,128)(2,1)} custom-call(s32[1,4]{1,0:T(1,128)} %structure_hbm.1, bf16[256,128]{1,0:T(8,128)(2,1)} %sigma_hbm.1), custom_call_target="tpu_custom_call" | custom-call | tf_op jit(solution)/shard_map/deal/pallas_call | solution.py:174
  2.4 0.0 copy-start
  2.4 0.0 copy-start.1
  2.4 42.0 %all_to_all.10.own = bf16[256,8,128]{2,1,0:T(8,128)(2,1)S(1)} all-to-all(bf16[256,8,128]{2,1,0:T(8,128)(2,1)} %deal.1), channel_id=1, replica_groups=mesh['y'=8,'xh'=2,'z'=8,'xl'=2,'c'=2] {'y','xh','z','xl'}, dimensions={0} | all-to-all | bytes 1048576 | tf_op jit(solution)/shard_map/all_to_all | solution.py:188
  44.4 1.9 %collective-permute-start = (bf16[256,8,128]{2,1,0:T(8,128)(2,1)S(1)}, bf16[256,8,128]{2,1,0:T(8,128)(2,1)S(1)}, u32[]{:S(2)}, u32[]{:S(2)}) collective-permute-start(bf16[256,8,128]{2,1,0:T(8,128)(2,1)S(1)} %all_to_all.10.own), channel_id=1, source_target_pairs={{0,1},{1,0},{2,3},{3,2},{4,5},{5,4},{6,7},{7,6},{8,9},{9,8},{10,11... | collective-permute-start | bytes 1572872 | tf_op jit(solution)/shard_map/ppermute | solution.py:190
  46.4 0.5 fusion
  46.9 0.1 reshape.8.names
  47.0 1.3 %collective-permute-done.other = bf16[256,8,128]{2,1,0:T(8,128)(2,1)S(1)} collective-permute-done((bf16[256,8,128]{2,1,0:T(8,128)(2,1)S(1)}, bf16[256,8,128]{2,1,0:T(8,128)(2,1)S(1)}, u32[]{:S(2)}, u32[]{:S(2)}) %collective-permute-start) | collective-permute-done | bytes 524320 | tf_op jit(solution)/shard_map/ppermute | solution.py:190
  48.2 1.5 %pick.1 = (bf16[64,64,128]{2,1,0:T(8,128)(2,1)S(1)}, f32[8,128]{1,0:T(8,128)S(1)}) custom-call(s32[1024]{0:T(1024)S(1)} %reshape.8.names, bf16[256,8,128]{2,1,0:T(8,128)(2,1)S(1)} %all_to_all.10.own, bf16[256,8,128]{2,1,0:T(8,128)(2,1)S(1)} %collective-permute-done.other), custom_call_target="tpu_custom_call" | custom-call | tf_op jit(solution)/shard_map/pick/pallas_call | solution.py:192
  49.8 36.1 %all_to_all.11.picked = bf16[64,64,128]{2,1,0:T(8,128)(2,1)S(1)} all-to-all(bf16[64,64,128]{2,1,0:T(8,128)(2,1)S(1)} %get-tuple-element.4), channel_id=1, replica_groups=mesh['y'=8,'xh'=2,'z'=8,'xl'=2,'c'=2] {'y','z'}, dimensions={0} | all-to-all | bytes 2097152 | tf_op jit(solution)/shard_map/all_to_all | solution.py:207
  85.9 0.0 copy-done
  85.9 0.0 copy-done.1
  85.9 4.1 %product.1 = (bf16[1,1024,1024]{2,1,0:T(8,128)(2,1)}, f32[1,1024]{1,0:T(1,128)}) custom-call(bf16[64,64,128]{2,1,0:T(8,128)(2,1)S(1)} %all_to_all.11.picked, f32[8,128]{1,0:T(8,128)S(1)} %get-tuple-element.5.far, bf16[1,1024,1024]{2,1,0:T(8,128)(2,1)S(1)} %copy-done, f32[1,1024]{1,0:T(1,128)S(1)} %copy-done.1), custom_call_target="tpu_custom_call" | custom-call | tf_op jit(solution)/shard_map/product/pallas_call | solution.py:209
Async XLA Ops:
  2.4 83.5 %copy-start = (bf16[1,1024,1024]{2,1,0:T(8,128)(2,1)S(1)}, bf16[1,1024,1024]{2,1,0:T(8,128)(2,1)}, u32[]{:S(2)}) copy-start(bf16[1,1024,1024]{2,1,0:T(8,128)(2,1)} %factor.1) | copy-start | bytes 6291460
  2.4 83.5 %copy-start.1 = (f32[1,1024]{1,0:T(1,128)S(1)}, f32[1,1024]{1,0:T(1,128)}, u32[]{:S(2)}) copy-start(f32[1,1024]{1,0:T(1,128)} %diag.1) | copy-start | bytes 12292
  44.4 3.8 %collective-permute-start = (bf16[256,8,128]{2,1,0:T(8,128)(2,1)S(1)}, bf16[256,8,128]{2,1,0:T(8,128)(2,1)S(1)}, u32[]{:S(2)}, u32[]{:S(2)}) collective-permute-start(bf16[256,8,128]{2,1,0:T(8,128)(2,1)S(1)} %all_to_all.10.own), channel_id=1, source_target_pairs={{0,1},{1,0},{2,3},{3,2},{4,5},{5,4},{6,7},{7,6},{8,9},{9,8},{10,11... | collective-permute-start | bytes 1572872 | tf_op jit(solution)/shard_map/ppermute | solution.py:190

commit v4 on v3

v4 whole, which is shorter than its diff:
```python
import jax
import jax.numpy as jnp
from jax import lax
from jax.experimental import pallas as pl
from jax.experimental.pallas import tpu as pltpu
from jax.sharding import Mesh, PartitionSpec as P

Y, XH, Z, XL, C = 8, 2, 8, 2, 2
AXES = ("y", "xh", "z", "xl", "c")
CHIPS = ("y", "xh", "z", "xl")
PLANE = ("y", "z")
NB = 16
NU = Y * Z
S = 4
PAIRS = [(k, l) for k in range(S) for l in range(k + 1, S)]
ROWS = 8 * len(PAIRS) + 4 * S


def iota(shape, dim):
    return lax.broadcasted_iota(jnp.int32, shape, dim)


def apart(shape):
    return (iota(shape, len(shape) - 1) - iota(shape, len(shape) - 2)) & 127


def kept(distance, low):
    return ((distance - low) & 127) < 64


def deal_kernel(structure_hbm, sigma_hbm, dealt, structure, sigma, out, sems, out_sems):
    copies = [
        pltpu.make_async_copy(structure_hbm, structure, sems.at[0]),
        pltpu.make_async_copy(sigma_hbm, sigma, sems.at[1]),
    ]
    for copy in copies:
        copy.start()
    for copy in copies:
        copy.wait()
    y_me, xh_me, z_me, xl_me, core = (lax.axis_index(a) for a in AXES)
    r, b = y_me * XH + xh_me, z_me * XL + xl_me
    lane, row = iota((8, 128), 1), iota((8, 128), 0)
    extra = jnp.zeros((8, 128), jnp.float32)
    for k in range(S):
        extra = jnp.where(lane == k, structure[0, k].astype(jnp.float32), extra)
    start = pl.multiple_of(128 * core, 128)
    square = sigma[pl.ds(start, 128), :].astype(jnp.float32)
    far = jnp.where(apart((128, 128)) == 64, square, 0.0)
    extra = jnp.where(row == 3, jnp.sum(far, axis=0, keepdims=True), extra)
    first = (lane < 64) == (core == 0)
    for v in range(NU // 2):
        tile = sigma[pl.ds(8 * v, 8), :].astype(jnp.float32)
        low = jnp.where(r == b, (v // 16 > core).astype(jnp.int32), (r > b).astype(jnp.int32))
        keep = kept(lane - row - 8 * v, low)
        tile = jnp.where(keep, tile, pltpu.roll(tile, 64, 1))
        tile = jnp.where(first, tile, pltpu.roll(tile, 6, 0))
        for odd in range(2):
            part = pltpu.roll(tile, 4, 0) if odd else tile
            part = jnp.where(row < 2, part, extra)[:4].astype(jnp.bfloat16)
            y, z = divmod(2 * v + odd, Z)
            for xh in range(XH):
                for xl in range(XL):
                    out[((y * XH + xh) * Z + z) * XL + xl] = part
        if z == Z - 1:
            part = pl.ds(y * XH * Z * XL, XH * Z * XL)
            copies.append(
                pltpu.make_async_copy(out.at[part], dealt.at[part], out_sems.at[y])
            )
            copies[-1].start()
    for copy in copies[2:]:
        copy.wait()


def pick_kernel(names, own, other, out, far, slices):
    y_me, xh, z_me, xl, core = (lax.axis_index(a) for a in AXES)
    mine = (((y_me * XH + xh) * Z + z_me) * XL + xl) * S

    def merge(left, right):
        def step(r, carry):
            parts = []
            for at in ((r, slice(None)), (slice(None), r)):
                one = left[at][:, :2].astype(jnp.float32)
                two = right[at][:, :2].astype(jnp.float32)
                west = iota(one.shape, 2) < 64
                parts += [jnp.where(west, one, two), jnp.where(west, two, one)]
            slices[r] = jnp.concatenate(parts, axis=1).astype(jnp.bfloat16)
            return carry

        lax.fori_loop(0, NB, step, 0)
        for k in range(S):
            at = names[mine + k]
            for g, half in enumerate((left, right)):
                far[4 * g + k : 4 * g + k + 1, :] = half[at, at].astype(jnp.float32)[3:4]

    @pl.when(core == 0)
    def _():
        merge(own, other)

    @pl.when(core != 0)
    def _():
        merge(other, own)

    def pick(y, carry):
        first = ((y * XH + xh) * Z * XL + xl) * S
        for z in range(Z):
            name = [names[first + z * XL * S + k] for k in range(S)]
            for p, (k, l) in enumerate(PAIRS):
                out[y * Z + z, pl.ds(8 * p, 8), :] = slices[name[k], name[l]]
            for k in range(S):
                rows = pl.ds(8 * len(PAIRS) + 4 * k, 4)
                out[y * Z + z, rows, :] = slices[name[k], name[k], pl.ds(0, 4), :]
        return carry

    lax.fori_loop(0, Y, pick, 0)


def unfold(picked, p):
    part = picked[:, pl.ds(8 * p, 8), :].astype(jnp.float32)
    turned = pltpu.roll(part, 4, 1)
    part = part.reshape(NU // 2, 2, 8, 128)
    turned = turned.reshape(NU // 2, 2, 8, 128)
    top = iota((NU // 2, 8, 128), 1) < 4
    first = (iota((256, 128), 1) < 64) == (iota((256, 128), 0) % 4 < 2)
    result = []
    for half in (
        jnp.where(top, part[:, 0], turned[:, 1]),
        jnp.where(top, turned[:, 0], part[:, 1]),
    ):
        half = half.reshape(256, 128)
        swapped = pltpu.roll(half, 64, 1).astype(jnp.bfloat16)
        half = half.astype(jnp.bfloat16)
        result.append((jnp.where(first, half, swapped), jnp.where(first, swapped, half)))
    return result


def quarter(half, g, h):
    return half[h][128 * g : 128 * g + 128]


def product_kernel(
    structure, picked, far, factor, diag, off, variance, gram, staged, sems
):
    total = diag[...]
    copies = []
    gap = apart((128, 128))
    for k in range(S):
        rows = pl.ds(256 * k, 256)
        for l in range(k, S):
            if l == k:
                if k % 2 == 0:
                    pair = unfold(picked, len(PAIRS) + k // 2)
                one = two = pair[k % 2]
            else:
                one, two = unfold(picked, PAIRS.index((k, l)))
                low = (structure[0, k] > structure[0, l]).astype(jnp.int32)
            for g in range(2):
                for h in range(2):
                    keep = kept(gap, int(g > h) if l == k else low)
                    value = jnp.where(keep, quarter(one, g, h), quarter(two, h, g).T)
                    if l == k and g == h:
                        spare = jnp.broadcast_to(far[pl.ds(4 * g + k, 1), :], value.shape)
                        value = jnp.where(gap == 64, spare.astype(jnp.bfloat16), value)
                    down, across = pl.ds(256 * k + 128 * g, 128), pl.ds(256 * l + 128 * h, 128)
                    gram[down, across] = value
                    if l > k:
                        gram[across, down] = value.T
        minus = jnp.dot(gram[rows, :], factor[0], preferred_element_type=jnp.float32)
        staged[k] = (-minus).astype(jnp.bfloat16)
        copies.append(pltpu.make_async_copy(staged.at[k], off.at[0, rows], sems.at[k]))
        copies[k].start()
        total += jnp.sum(
            factor[0, rows, :].astype(jnp.float32) * minus, axis=0, keepdims=True
        )
    variance[...] = total
    for copy in copies:
        copy.wait()


def body(sigma, structure, factor, diag):
    vmem, smem = pltpu.VMEM, pltpu.SMEM
    whole = pl.BlockSpec(memory_space=vmem)
    scalars = pl.BlockSpec(memory_space=smem)
    anywhere = pl.BlockSpec(memory_space=pl.ANY)

    dealt = pl.pallas_call(
        deal_kernel,
        out_shape=jax.ShapeDtypeStruct((NB * NB, 4, 128), jnp.bfloat16),
        in_specs=[anywhere, anywhere],
        out_specs=anywhere,
        scratch_shapes=[
            smem(structure.shape, jnp.int32),
            vmem(sigma.shape, jnp.bfloat16),
            vmem((NB * NB, 4, 128), jnp.bfloat16),
            pltpu.SemaphoreType.DMA((2,)),
            pltpu.SemaphoreType.DMA((Y,)),
        ],
        name="deal",
    )(structure, sigma)
    own = lax.all_to_all(dealt, CHIPS, 0, 0, tiled=True)
    flip = [(d, d ^ 1) for d in range(2 * NB * NB)]
    other = lax.ppermute(own, AXES, flip)
    grid = (NB, NB, 4, 128)
    names = own[:, 2, :S].astype(jnp.int32).reshape(NB * NB * S)
    chosen, far = pl.pallas_call(
        pick_kernel,
        out_shape=(
            jax.ShapeDtypeStruct((NU, ROWS, 128), jnp.bfloat16),
            jax.ShapeDtypeStruct((8, 128), jnp.float32),
        ),
        in_specs=[scalars, whole, whole],
        out_specs=(whole, whole),
        scratch_shapes=[vmem((NB, NB, 8, 128), jnp.bfloat16)],
        compiler_params=pltpu.CompilerParams(vmem_limit_bytes=6 << 20),
        name="pick",
    )(names, own.reshape(grid), other.reshape(grid))
    picked = lax.all_to_all(chosen, PLANE, 0, 0, tiled=True)

    off, variance = pl.pallas_call(
        product_kernel,
        out_shape=(
            jax.ShapeDtypeStruct(factor.shape, jnp.bfloat16),
            jax.ShapeDtypeStruct(diag.shape, jnp.float32),
        ),
        in_specs=[scalars, whole, whole, whole, whole],
        out_specs=(anywhere, whole),
        scratch_shapes=[
            vmem((1024, 1024), jnp.bfloat16),
            vmem((S, 256, 1024), jnp.bfloat16),
            pltpu.SemaphoreType.DMA((S,)),
        ],
        compiler_params=pltpu.CompilerParams(vmem_limit_bytes=24 << 20),
        name="product",
    )(structure, picked, far, factor, diag)
    return off, variance


def solution(mesh):
    fine = Mesh(mesh.devices.reshape(Y, XH, Z, XL, C), AXES)
    return jax.shard_map(
        body,
        mesh=fine,
        in_specs=(
            P(("y", "xh"), ("z", "xl", "c")),
            P(AXES, None),
            P(AXES, None, None),
            P(AXES, None),
        ),
        out_specs=(P(AXES, None, None), P(AXES, None)),
        check_vma=False,
    )
```

time: 90.3 us -> 86.2 us (0.955)
  blocking collectives: 78.2 us -> 72.8 us
  Pallas kernels: 7.35 us -> 9.08 us
    all_to_all x1, blocking collectives: 42 us -> 36.5 us  [body(): own = lax.all_to_all(dealt, CHIPS, 0, 0, tiled=True)]
    pallas_call x1, Pallas kernels: 4.11 us -> 5.27 us  [body(): pl.pallas_call(product_kernel, out_shape=(jax.ShapeDtypeStruct(factor.sha...]
where the time goes in v4:
time: 86.2 us; the launch traced here: 85.9 us
  blocking collectives  72.8 us (84%)
  Pallas kernels  9.08 us (11%)
  starting transfers between devices  1.91 us (2%)
  waiting for transfers between devices  0.88 us (1%)
    all_to_all x1, blocking collectives, body(): own = lax.all_to_all(dealt, CHIPS, 0, 0, tiled=True)  36.5 us
    all_to_all x1, blocking collectives, body(): picked = lax.all_to_all(chosen, PLANE, 0, 0, tiled=True)  36.2 us
    pallas_call x1, Pallas kernels, body(): pl.pallas_call(product_kernel, out_shape=(jax.ShapeDtypeStruct(factor.sha...  5.27 us
    pallas_call x1, Pallas kernels, body(): pl.pallas_call(pick_kernel, out_shape=(jax.ShapeDtypeStruct((NU, ROWS, 12...  1.95 us
    ppermute x1, starting transfers between devices, body(): other = lax.ppermute(own, AXES, flip)  1.91 us
    pallas_call x1, Pallas kernels, body(): pl.pallas_call(deal_kernel, out_shape=jax.ShapeDtypeStruct((NB * NB, 4, 1...  1.85 us
  transfers between devices with their start and end apart: 1, of which 1 were waited for; matrix products, arithmetic and copies ran while one was open for 1% of the time, Pallas kernels for 0%

profile of v4, /device:TPU:16, one launch (start us, length us, event | category | flops | bytes accessed | tf_op | source)
XLA Modules:
  0.0 85.9 jit_solution(8882119033571771841)
XLA Ops:
  0.6 0.0 copy-start.2
  0.6 0.0 copy-start.1
  0.7 0.0 copy-start
  0.7 1.9 %deal.1 = bf16[256,4,128]{2,1,0:T(4,128)(2,1)} custom-call(s32[1,4]{1,0:T(1,128)} %structure.1, bf16[256,128]{1,0:T(8,128)(2,1)} %sigma_hbm.1), custom_call_target="tpu_custom_call" | custom-call | tf_op jit(solution)/shard_map/deal/pallas_call | solution.py:185
  2.5 36.5 %all_to_all.10 = bf16[256,4,128]{2,1,0:T(4,128)(2,1)S(1)} all-to-all(bf16[256,4,128]{2,1,0:T(4,128)(2,1)} %deal.1), channel_id=1, replica_groups=mesh['y'=8,'xh'=2,'z'=8,'xl'=2,'c'=2] {'y','xh','z','xl'}, dimensions={0} | all-to-all | bytes 524288 | tf_op jit(solution)/shard_map/all_to_all | solution.py:199
  39.0 1.9 %collective-permute-start = (bf16[256,4,128]{2,1,0:T(4,128)(2,1)S(1)}, bf16[256,4,128]{2,1,0:T(4,128)(2,1)S(1)}, u32[]{:S(2)}, u32[]{:S(2)}) collective-permute-start(bf16[256,4,128]{2,1,0:T(4,128)(2,1)S(1)} %all_to_all.10), channel_id=1, source_target_pairs={{0,1},{1,0},{2,3},{3,2},{4,5},{5,4},{6,7},{7,6},{8,9},{9,8},{10,11... | collective-permute-start | bytes 786440 | tf_op jit(solution)/shard_map/ppermute | solution.py:201
  41.0 0.5 fusion
  41.4 0.1 reshape.16.names
  41.6 0.9 %collective-permute-done = bf16[256,4,128]{2,1,0:T(4,128)(2,1)S(1)} collective-permute-done((bf16[256,4,128]{2,1,0:T(4,128)(2,1)S(1)}, bf16[256,4,128]{2,1,0:T(4,128)(2,1)S(1)}, u32[]{:S(2)}, u32[]{:S(2)}) %collective-permute-start) | collective-permute-done | bytes 262176 | tf_op jit(solution)/shard_map/ppermute | solution.py:201
  42.5 2.0 %pick.1 = (bf16[64,64,128]{2,1,0:T(8,128)(2,1)S(1)}, f32[8,128]{1,0:T(8,128)S(1)}) custom-call(s32[1024]{0:T(1024)S(1)} %reshape.16.names, bf16[16,16,4,128]{3,2,1,0:T(4,128)(2,1)S(1)} %bitcast.2, bf16[16,16,4,128]{3,2,1,0:T(4,128)(2,1)S(1)} %bitcast.3), custom_call_target="tpu_custom_call" | custom-call | tf_op jit(solution)/shard_map/pick/pallas_call | solution.py:204
  44.4 36.2 %all_to_all.11.picked = bf16[64,64,128]{2,1,0:T(8,128)(2,1)S(1)} all-to-all(bf16[64,64,128]{2,1,0:T(8,128)(2,1)S(1)} %get-tuple-element.4), channel_id=1, replica_groups=mesh['y'=8,'xh'=2,'z'=8,'xl'=2,'c'=2] {'y','z'}, dimensions={0} | all-to-all | bytes 2097152 | tf_op jit(solution)/shard_map/all_to_all | solution.py:216
  80.7 0.0 copy-done.2
  80.7 0.0 copy-done.1
  80.7 0.0 copy-done
  80.7 5.3 %product.1 = (bf16[1,1024,1024]{2,1,0:T(8,128)(2,1)}, f32[1,1024]{1,0:T(1,128)}) custom-call(s32[1,4]{1,0:T(1,128)S(1)} %copy-done.2, bf16[64,64,128]{2,1,0:T(8,128)(2,1)S(1)} %all_to_all.11.picked, f32[8,128]{1,0:T(8,128)S(1)} %get-tuple-element.5.far, bf16[1,1024,1024]{2,1,0:T(8,128)(2,1)S(1)} %copy-done, f32[1,1024]{1,0:T(1,128)S(1)} %copy-done.1), custom_call_target="tpu_custom_call" | custom-call | tf_op jit(solution)/shard_map/product/pallas_call | solution.py:218
Async XLA Ops:
  0.6 80.0 %copy-start.2 = (s32[1,4]{1,0:T(1,128)S(1)}, s32[1,4]{1,0:T(1,128)}, u32[]{:S(2)}) copy-start(s32[1,4]{1,0:T(1,128)} %structure.1) | copy-start | bytes 52
  0.6 80.0 %copy-start.1 = (f32[1,1024]{1,0:T(1,128)S(1)}, f32[1,1024]{1,0:T(1,128)}, u32[]{:S(2)}) copy-start(f32[1,1024]{1,0:T(1,128)} %diag.1) | copy-start | bytes 12292
  0.7 80.0 %copy-start = (bf16[1,1024,1024]{2,1,0:T(8,128)(2,1)S(1)}, bf16[1,1024,1024]{2,1,0:T(8,128)(2,1)}, u32[]{:S(2)}) copy-start(bf16[1,1024,1024]{2,1,0:T(8,128)(2,1)} %factor.1) | copy-start | bytes 6291460
  39.0 3.4 %collective-permute-start = (bf16[256,4,128]{2,1,0:T(4,128)(2,1)S(1)}, bf16[256,4,128]{2,1,0:T(4,128)(2,1)S(1)}, u32[]{:S(2)}, u32[]{:S(2)}) collective-permute-start(bf16[256,4,128]{2,1,0:T(4,128)(2,1)S(1)} %all_to_all.10), channel_id=1, source_target_pairs={{0,1},{1,0},{2,3},{3,2},{4,5},{5,4},{6,7},{7,6},{8,9},{9,8},{10,11... | collective-permute-start | bytes 786440 | tf_op jit(solution)/shard_map/ppermute | solution.py:201

commit v5 on v4

v5 whole, which is shorter than its diff:
```python
import jax
import jax.numpy as jnp
from jax import lax
from jax.experimental import pallas as pl
from jax.experimental.pallas import tpu as pltpu
from jax.sharding import Mesh, PartitionSpec as P

SIZES = dict(yh=4, yl=2, xh=2, zh=4, zl=2, xl=2, c=2)
AXES = tuple(SIZES)
CHIPS = AXES[:-1]
NEAR = ("yl", "xh", "zl", "xl")
NB = 16
NU = 16
S = 4
PAIRS = [(k, l) for k in range(S) for l in range(k + 1, S)]
ORDER = [q for k, l in PAIRS for q in ((k, l), (l, k))] + [(k, k) for k in range(S)]


def iota(shape, dim):
    return lax.broadcasted_iota(jnp.int32, shape, dim)


def apart(shape):
    return (iota(shape, len(shape) - 1) - iota(shape, len(shape) - 2)) & 127


def kept(distance, low):
    return ((distance - low) & 127) < 64


def place():
    yh, yl, xh, zh, zl, xl, core = (lax.axis_index(a) for a in AXES)
    return 4 * yh + 2 * yl + xh, 4 * zh + 2 * zl + xl, core


def deal_kernel(structure_hbm, sigma_hbm, dealt, structure, sigma, out, sems, out_sems):
    copies = [
        pltpu.make_async_copy(structure_hbm, structure, sems.at[0]),
        pltpu.make_async_copy(sigma_hbm, sigma, sems.at[1]),
    ]
    for copy in copies:
        copy.start()
    for copy in copies:
        copy.wait()
    r, b, core = place()
    lane, row = iota((8, 128), 1), iota((8, 128), 0)
    extra = jnp.zeros((8, 128), jnp.float32)
    for k in range(S):
        extra = jnp.where(lane == k, structure[0, k].astype(jnp.float32), extra)
    start = pl.multiple_of(128 * core, 128)
    square = sigma[pl.ds(start, 128), :].astype(jnp.float32)
    far = jnp.where(apart((128, 128)) == 64, square, 0.0)
    extra = jnp.where(row == 1, jnp.sum(far, axis=0, keepdims=True), extra)
    extra = extra[:2].astype(jnp.bfloat16)
    first = (lane < 64) == (core == 0)
    for u in range(NU):
        low = jnp.where(r == b, (u // 8 > core).astype(jnp.int32), (r > b).astype(jnp.int32))
        tiles = []
        for v in (2 * u, 2 * u + 1):
            tile = sigma[pl.ds(8 * v, 8), :].astype(jnp.float32)
            keep = kept(lane - row - 8 * v, low)
            tiles.append(jnp.where(keep, tile, pltpu.roll(tile, 64, 1)))
        tile = jnp.where(first, *tiles)
        for j in range(4):
            out[u // 4, u % 4, j] = tile[2 * j : 2 * j + 2].astype(jnp.bfloat16)
        out[u // 4, u % 4, 4] = extra
    spread = [
        pltpu.make_async_copy(out, dealt.at[yh, :, zh], out_sems.at[yh, zh])
        for yh in range(4)
        for zh in range(4)
    ]
    for copy in spread:
        copy.start()
    for copy in spread:
        copy.wait()


def pick_kernel(names, own, other, out, far):
    r_me, b_me, core = place()
    y0, z0 = r_me // 4 * 4, b_me // 4 * 4
    west = iota((8, 128), 1) < 64

    def run(left, right):
        mine = (r_me * NB + b_me) * S
        for k in range(S):
            at = names[mine + k]
            for g, half in enumerate((left, right)):
                far[4 * g + k : 4 * g + k + 1, :] = half[at, at, 4].astype(jnp.float32)[1:2]

        def step(t, carry):
            first = ((y0 + t // 4) * NB + z0 + t % 4) * S
            name = [names[first + k] for k in range(S)]
            for q, (k, l) in enumerate(ORDER):
                at = (name[k], name[l], pl.ds(0, 4))
                one = left[at].astype(jnp.float32).reshape(8, 128)
                two = right[at].astype(jnp.float32).reshape(8, 128)
                both = [jnp.where(west, one, two), jnp.where(west, two, one)]
                rows = pl.ds(16 * q, 16)
                out[t, rows, :] = jnp.concatenate(both, axis=0).astype(jnp.bfloat16)
            return carry

        lax.fori_loop(0, NU, step, 0)

    @pl.when(core == 0)
    def _():
        run(own, other)

    @pl.when(core != 0)
    def _():
        run(other, own)


def unfold(picked, q):
    half = picked[:, pl.ds(16 * q, 16), :].reshape(256, 128)
    swapped = pltpu.roll(half.astype(jnp.float32), 64, 1).astype(jnp.bfloat16)
    first = (iota((256, 128), 1) < 64) == (iota((256, 128), 0) % 16 < 8)
    return jnp.where(first, half, swapped), jnp.where(first, swapped, half)


def quarter(half, g, h):
    return half[h][128 * g : 128 * g + 128]


def product_kernel(
    structure, picked, far, factor, diag, off, variance, gram, staged, sems
):
    total = diag[...]
    copies = []
    gap = apart((128, 128))
    for k in range(S):
        rows = pl.ds(256 * k, 256)
        for l in range(k, S):
            if l == k:
                one = two = unfold(picked, ORDER.index((k, k)))
            else:
                one = unfold(picked, ORDER.index((k, l)))
                two = unfold(picked, ORDER.index((l, k)))
                low = (structure[0, k] > structure[0, l]).astype(jnp.int32)
            for g in range(2):
                for h in range(2):
                    keep = kept(gap, int(g > h) if l == k else low)
                    value = jnp.where(keep, quarter(one, g, h), quarter(two, h, g).T)
                    if l == k and g == h:
                        spare = jnp.broadcast_to(far[pl.ds(4 * g + k, 1), :], value.shape)
                        value = jnp.where(gap == 64, spare.astype(jnp.bfloat16), value)
                    down, across = pl.ds(256 * k + 128 * g, 128), pl.ds(256 * l + 128 * h, 128)
                    gram[down, across] = value
                    if l > k:
                        gram[across, down] = value.T
        minus = jnp.dot(gram[rows, :], factor[0], preferred_element_type=jnp.float32)
        staged[k] = (-minus).astype(jnp.bfloat16)
        copies.append(pltpu.make_async_copy(staged.at[k], off.at[0, rows], sems.at[k]))
        copies[k].start()
        total += jnp.sum(
            factor[0, rows, :].astype(jnp.float32) * minus, axis=0, keepdims=True
        )
    variance[...] = total
    for copy in copies:
        copy.wait()


def body(sigma, structure, factor, diag):
    vmem, smem = pltpu.VMEM, pltpu.SMEM
    whole = pl.BlockSpec(memory_space=vmem)
    scalars = pl.BlockSpec(memory_space=smem)
    anywhere = pl.BlockSpec(memory_space=pl.ANY)

    message = (5, 2, 128)
    dealt = pl.pallas_call(
        deal_kernel,
        out_shape=jax.ShapeDtypeStruct((4, 4, 4, 4) + message, jnp.bfloat16),
        in_specs=[anywhere, anywhere],
        out_specs=anywhere,
        scratch_shapes=[
            smem(structure.shape, jnp.int32),
            vmem(sigma.shape, jnp.bfloat16),
            vmem((4, 4) + message, jnp.bfloat16),
            pltpu.SemaphoreType.DMA((2,)),
            pltpu.SemaphoreType.DMA((4, 4)),
        ],
        name="deal",
    )(structure, sigma)
    own = lax.all_to_all(dealt.reshape((NB * NB,) + message), CHIPS, 0, 0, tiled=True)
    flip = [(d, d ^ 1) for d in range(2 * NB * NB)]
    other = lax.ppermute(own, AXES, flip)
    grid = (NB, NB) + message
    names = own[:, 4, 0, :S].astype(jnp.int32).reshape(NB * NB * S)
    chosen, far = pl.pallas_call(
        pick_kernel,
        out_shape=(
            jax.ShapeDtypeStruct((NU, 16 * len(ORDER), 128), jnp.bfloat16),
            jax.ShapeDtypeStruct((8, 128), jnp.float32),
        ),
        in_specs=[scalars, whole, whole],
        out_specs=(whole, whole),
        compiler_params=pltpu.CompilerParams(vmem_limit_bytes=6 << 20),
        name="pick",
    )(names, own.reshape(grid), other.reshape(grid))
    picked = lax.all_to_all(chosen, NEAR, 0, 0, tiled=True)

    off, variance = pl.pallas_call(
        product_kernel,
        out_shape=(
            jax.ShapeDtypeStruct(factor.shape, jnp.bfloat16),
            jax.ShapeDtypeStruct(diag.shape, jnp.float32),
        ),
        in_specs=[scalars, whole, whole, whole, whole],
        out_specs=(anywhere, whole),
        scratch_shapes=[
            vmem((1024, 1024), jnp.bfloat16),
            vmem((S, 256, 1024), jnp.bfloat16),
            pltpu.SemaphoreType.DMA((S,)),
        ],
        compiler_params=pltpu.CompilerParams(vmem_limit_bytes=24 << 20),
        name="product",
    )(structure, picked, far, factor, diag)
    return off, variance


def solution(mesh):
    fine = Mesh(mesh.devices.reshape(tuple(SIZES.values())), AXES)
    return jax.shard_map(
        body,
        mesh=fine,
        in_specs=(
            P(AXES[:3], AXES[3:]),
            P(AXES, None),
            P(AXES, None, None),
            P(AXES, None),
        ),
        out_specs=(P(AXES, None, None), P(AXES, None)),
        check_vma=False,
    )
```

time: 86.2 us -> 80.6 us (0.935)
  the two profiles are of different devices: /device:TPU:16 before, /device:TPU:1 now
where the time goes in v5:
time: 80.6 us; the launch traced here: 80.3 us
  blocking collectives  64.8 us (80%)
  Pallas kernels  8.72 us (11%)
  starting transfers between devices  4.49 us (6%)
  waiting for transfers between devices  1.15 us (1%)
    all_to_all x1, blocking collectives, body(): lax.all_to_all(dealt.reshape((NB * NB,) + message), CHIPS, 0, 0, tiled=True)  44.6 us
    all_to_all x1, blocking collectives, body(): picked = lax.all_to_all(chosen, NEAR, 0, 0, tiled=True)  20.1 us
    pallas_call x1, Pallas kernels, body(): pl.pallas_call(product_kernel, out_shape=(jax.ShapeDtypeStruct(factor.sha...  5.13 us
    ppermute x1, starting transfers between devices, body(): other = lax.ppermute(own, AXES, flip)  4.49 us
    pallas_call x1, Pallas kernels, body(): pl.pallas_call(deal_kernel, out_shape=jax.ShapeDtypeStruct((4, 4, 4, 4) +...  1.92 us
    pallas_call x1, Pallas kernels, body(): pl.pallas_call(pick_kernel, out_shape=(jax.ShapeDtypeStruct((NU, 16 * len...  1.68 us
  transfers between devices with their start and end apart: 1, of which 1 were waited for; matrix products, arithmetic and copies ran while one was open for 1% of the time, Pallas kernels for 0%

profile of v5, /device:TPU:1, one launch (start us, length us, event | category | flops | bytes accessed | tf_op | source)
XLA Modules:
  0.0 80.3 jit_solution(8806699534738754098)
XLA Ops:
  0.6 1.9 %deal.1 = bf16[4,4,4,4,5,2,128]{6,5,4,3,2,1,0:T(2,128)(2,1)} custom-call(s32[1,4]{1,0:T(1,128)} %structure.1, bf16[256,128]{1,0:T(8,128)(2,1)} %sigma_hbm.1), custom_call_target="tpu_custom_call" | custom-call | tf_op jit(solution)/shard_map/deal/pallas_call | solution.py:169
  2.6 44.6 %all_to_all.10 = bf16[256,5,2,128]{3,2,1,0:T(2,128)(2,1)S(1)} all-to-all(bf16[256,5,2,128]{3,2,1,0:T(2,128)(2,1)} %bitcast.5), channel_id=1, replica_groups=mesh['yh'=4,'yl'=2,'xh'=2,'zh'=4,'zl'=2,'xl'=2,'c'=2] {'yh','yl','xh','z..., dimensions={0} | all-to-all | bytes 1310720 | tf_op jit(solution)/shard_map/all_to_all | solution.py:183
  47.2 0.0 copy-start
  47.2 0.0 copy-start.1
  47.2 0.0 copy-start.2
  47.2 4.5 %collective-permute-start = (bf16[256,5,2,128]{3,2,1,0:T(2,128)(2,1)S(1)}, bf16[256,5,2,128]{3,2,1,0:T(2,128)(2,1)S(1)}, u32[]{:S(2)}, u32[]{:S(2)}) collective-permute-start(bf16[256,5,2,128]{3,2,1,0:T(2,128)(2,1)S(1)} %all_to_all.10), channel_id=1, source_target_pairs={{0,1},{1,0},{2,3},{3,2},{4,5},{5,4},{6,7},{7,6},{8,9},{9,8},{10,11... | collective-permute-start | bytes 1966088 | tf_op jit(solution)/shard_map/ppermute | solution.py:185
  51.7 0.4 fusion
  52.1 0.1 reshape.20.names
  52.2 1.2 %collective-permute-done = bf16[256,5,2,128]{3,2,1,0:T(2,128)(2,1)S(1)} collective-permute-done((bf16[256,5,2,128]{3,2,1,0:T(2,128)(2,1)S(1)}, bf16[256,5,2,128]{3,2,1,0:T(2,128)(2,1)S(1)}, u32[]{:S(2)}, u32[]{:S(2)}) %collective-permute-start) | collective-permute-done | bytes 655392 | tf_op jit(solution)/shard_map/ppermute | solution.py:185
  53.4 1.7 %pick.1 = (bf16[16,256,128]{2,1,0:T(8,128)(2,1)S(1)}, f32[8,128]{1,0:T(8,128)S(1)}) custom-call(s32[1024]{0:T(1024)S(1)} %reshape.20.names, bf16[16,16,5,2,128]{4,3,2,1,0:T(2,128)(2,1)S(1)} %bitcast.3, bf16[16,16,5,2,128]{4,3,2,1,0:T(2,128)(2,1)S(1)} %bitcast.4), custom_call_target="tpu_custom_call" | custom-call | tf_op jit(solution)/shard_map/pick/pallas_call | solution.py:188
  55.1 20.1 %all_to_all.11.picked = bf16[16,256,128]{2,1,0:T(8,128)(2,1)S(1)} all-to-all(bf16[16,256,128]{2,1,0:T(8,128)(2,1)S(1)} %get-tuple-element.4), channel_id=1, replica_groups=mesh['yh'=4,'yl'=2,'xh'=2,'zh'=4,'zl'=2,'xl'=2,'c'=2] {'yl','xh','zl','xl'}, dimensions={0} | all-to-all | bytes 2097152 | tf_op jit(solution)/shard_map/all_to_all | solution.py:199
  75.2 0.0 copy-done
  75.2 0.0 copy-done.1
  75.2 0.0 copy-done.2
  75.2 5.1 %product.1 = (bf16[1,1024,1024]{2,1,0:T(8,128)(2,1)}, f32[1,1024]{1,0:T(1,128)}) custom-call(s32[1,4]{1,0:T(1,128)S(1)} %copy-done.2, bf16[16,256,128]{2,1,0:T(8,128)(2,1)S(1)} %all_to_all.11.picked, f32[8,128]{1,0:T(8,128)S(1)} %get-tuple-element.5.far, bf16[1,1024,1024]{2,1,0:T(8,128)(2,1)S(1)} %copy-done, f32[1,1024]{1,0:T(1,128)S(1)} %copy-done.1), custom_call_target="tpu_custom_call" | custom-call | tf_op jit(solution)/shard_map/product/pallas_call | solution.py:201
Async XLA Ops:
  47.2 28.0 %copy-start = (bf16[1,1024,1024]{2,1,0:T(8,128)(2,1)S(1)}, bf16[1,1024,1024]{2,1,0:T(8,128)(2,1)}, u32[]{:S(2)}) copy-start(bf16[1,1024,1024]{2,1,0:T(8,128)(2,1)} %factor.1) | copy-start | bytes 6291460
  47.2 28.0 %copy-start.1 = (f32[1,1024]{1,0:T(1,128)S(1)}, f32[1,1024]{1,0:T(1,128)}, u32[]{:S(2)}) copy-start(f32[1,1024]{1,0:T(1,128)} %diag.1) | copy-start | bytes 12292
  47.2 28.0 %copy-start.2 = (s32[1,4]{1,0:T(1,128)S(1)}, s32[1,4]{1,0:T(1,128)}, u32[]{:S(2)}) copy-start(s32[1,4]{1,0:T(1,128)} %structure.1) | copy-start | bytes 52
  47.2 6.2 %collective-permute-start = (bf16[256,5,2,128]{3,2,1,0:T(2,128)(2,1)S(1)}, bf16[256,5,2,128]{3,2,1,0:T(2,128)(2,1)S(1)}, u32[]{:S(2)}, u32[]{:S(2)}) collective-permute-start(bf16[256,5,2,128]{3,2,1,0:T(2,128)(2,1)S(1)} %all_to_all.10), channel_id=1, source_target_pairs={{0,1},{1,0},{2,3},{3,2},{4,5},{5,4},{6,7},{7,6},{8,9},{9,8},{10,11... | collective-permute-start | bytes 1966088 | tf_op jit(solution)/shard_map/ppermute | solution.py:185

commit v6 on v5

--- a/solution.py
+++ b/solution.py
@@ -12,6 +12,7 @@
 NB = 16
 NU = 16
 S = 4
+ENDS, RUNS = (1, 4), (1, 2)
 PAIRS = [(k, l) for k in range(S) for l in range(k + 1, S)]
 ORDER = [q for k, l in PAIRS for q in ((k, l), (l, k))] + [(k, k) for k in range(S)]
 
@@ -48,7 +49,7 @@
     for k in range(S):
         extra = jnp.where(lane == k, structure[0, k].astype(jnp.float32), extra)
     start = pl.multiple_of(128 * core, 128)
-    square = sigma[pl.ds(start, 128), :].astype(jnp.float32)
+    square = -sigma[pl.ds(start, 128), :].astype(jnp.float32)
     far = jnp.where(apart((128, 128)) == 64, square, 0.0)
     extra = jnp.where(row == 1, jnp.sum(far, axis=0, keepdims=True), extra)
     extra = extra[:2].astype(jnp.bfloat16)
@@ -57,7 +58,7 @@
         low = jnp.where(r == b, (u // 8 > core).astype(jnp.int32), (r > b).astype(jnp.int32))
         tiles = []
         for v in (2 * u, 2 * u + 1):
-            tile = sigma[pl.ds(8 * v, 8), :].astype(jnp.float32)
+            tile = -sigma[pl.ds(8 * v, 8), :].astype(jnp.float32)
             keep = kept(lane - row - 8 * v, low)
             tiles.append(jnp.where(keep, tile, pltpu.roll(tile, 64, 1)))
         tile = jnp.where(first, *tiles)
@@ -87,19 +88,21 @@
             for g, half in enumerate((left, right)):
                 far[4 * g + k : 4 * g + k + 1, :] = half[at, at, 4].astype(jnp.float32)[1:2]
 
-        def step(t, carry):
-            first = ((y0 + t // 4) * NB + z0 + t % 4) * S
-            name = [names[first + k] for k in range(S)]
-            for q, (k, l) in enumerate(ORDER):
-                at = (name[k], name[l], pl.ds(0, 4))
-                one = left[at].astype(jnp.float32).reshape(8, 128)
-                two = right[at].astype(jnp.float32).reshape(8, 128)
-                both = [jnp.where(west, one, two), jnp.where(west, two, one)]
-                rows = pl.ds(16 * q, 16)
-                out[t, rows, :] = jnp.concatenate(both, axis=0).astype(jnp.bfloat16)
+        def step(i, carry):
+            for j in range(4):
+                t = 4 * i + j
+                first = ((y0 + i) * NB + z0 + j) * S
+                name = [names[first + k] for k in range(S)]
+                for q, (k, l) in enumerate(ORDER):
+                    at = (name[k], name[l], pl.ds(0, 4))
+                    one = left[at].astype(jnp.float32).reshape(8, 128)
+                    two = right[at].astype(jnp.float32).reshape(8, 128)
+                    both = [jnp.where(west, one, two), jnp.where(west, two, one)]
+                    rows = pl.ds(16 * q, 16)
+                    out[t, rows, :] = jnp.concatenate(both, axis=0).astype(jnp.bfloat16)
             return carry
 
-        lax.fori_loop(0, NU, step, 0)
+        lax.fori_loop(0, NU // 4, step, 0)
 
     @pl.when(core == 0)
     def _():
@@ -124,7 +127,6 @@
 def product_kernel(
     structure, picked, far, factor, diag, off, variance, gram, staged, sems
 ):
-    total = diag[...]
     copies = []
     gap = apart((128, 128))
     for k in range(S):
@@ -147,14 +149,25 @@
                     gram[down, across] = value
                     if l > k:
                         gram[across, down] = value.T
-        minus = jnp.dot(gram[rows, :], factor[0], preferred_element_type=jnp.float32)
-        staged[k] = (-minus).astype(jnp.bfloat16)
-        copies.append(pltpu.make_async_copy(staged.at[k], off.at[0, rows], sems.at[k]))
-        copies[k].start()
-        total += jnp.sum(
-            factor[0, rows, :].astype(jnp.float32) * minus, axis=0, keepdims=True
-        )
-    variance[...] = total
+        if k + 1 not in ENDS:
+            continue
+        start = max((end for end in ENDS if end <= k), default=0)
+        rows = pl.ds(256 * start, 256 * (k + 1 - start))
+        runs = RUNS[ENDS.index(k + 1)]
+        for run in range(runs):
+            columns = pl.ds(1024 // runs * run, 1024 // runs)
+            part = factor[0, :, columns]
+            product = jnp.dot(gram[rows, :], part, preferred_element_type=jnp.float32)
+            staged[rows, columns] = product.astype(jnp.bfloat16)
+            copies.append(
+                pltpu.make_async_copy(
+                    staged.at[rows, columns], off.at[0, rows, columns], sems.at[len(copies)]
+                )
+            )
+            copies[-1].start()
+            mine = factor[0, rows, columns].astype(jnp.float32)
+            total = jnp.sum(mine * product, axis=0, keepdims=True)
+            variance[:, columns] = (diag if start == 0 else variance)[:, columns] - total
     for copy in copies:
         copy.wait()
 
@@ -208,8 +221,8 @@
         out_specs=(anywhere, whole),
         scratch_shapes=[
             vmem((1024, 1024), jnp.bfloat16),
-            vmem((S, 256, 1024), jnp.bfloat16),
-            pltpu.SemaphoreType.DMA((S,)),
+            vmem((1024, 1024), jnp.bfloat16),
+            pltpu.SemaphoreType.DMA((sum(RUNS),)),
         ],
         compiler_params=pltpu.CompilerParams(vmem_limit_bytes=24 << 20),
         name="product",

time: 80.6 us -> 80.4 us (level)
  no operation moved by 1% of the time
where the time goes in v6:
time: 80.4 us; the launch traced here: 80.1 us
  blocking collectives  64.8 us (81%)
  Pallas kernels  8.46 us (11%)
  starting transfers between devices  4.49 us (6%)
  waiting for transfers between devices  1.15 us (1%)
    all_to_all x1, blocking collectives, body(): lax.all_to_all(dealt.reshape((NB * NB,) + message), CHIPS, 0, 0, tiled=True)  44.6 us
    all_to_all x1, blocking collectives, body(): picked = lax.all_to_all(chosen, NEAR, 0, 0, tiled=True)  20.1 us
    pallas_call x1, Pallas kernels, body(): pl.pallas_call(product_kernel, out_shape=(jax.ShapeDtypeStruct(factor.sha...  5.11 us
    ppermute x1, starting transfers between devices, body(): other = lax.ppermute(own, AXES, flip)  4.49 us
    pallas_call x1, Pallas kernels, body(): pl.pallas_call(deal_kernel, out_shape=jax.ShapeDtypeStruct((4, 4, 4, 4) +...  1.92 us
  transfers between devices with their start and end apart: 1, of which 1 were waited for; matrix products, arithmetic and copies ran while one was open for 1% of the time, Pallas kernels for 0%

profile of v6, /device:TPU:1, one launch (start us, length us, event | category | flops | bytes accessed | tf_op | source)
XLA Modules:
  0.0 80.1 jit_solution(616943097324967536)
XLA Ops:
  0.6 1.9 %deal.1 = bf16[4,4,4,4,5,2,128]{6,5,4,3,2,1,0:T(2,128)(2,1)} custom-call(s32[1,4]{1,0:T(1,128)} %structure.1, bf16[256,128]{1,0:T(8,128)(2,1)} %sigma_hbm.1), custom_call_target="tpu_custom_call" | custom-call | tf_op jit(solution)/shard_map/deal/pallas_call | solution.py:182
  2.6 44.6 %all_to_all.10 = bf16[256,5,2,128]{3,2,1,0:T(2,128)(2,1)S(1)} all-to-all(bf16[256,5,2,128]{3,2,1,0:T(2,128)(2,1)} %bitcast.5), channel_id=1, replica_groups=mesh['yh'=4,'yl'=2,'xh'=2,'zh'=4,'zl'=2,'xl'=2,'c'=2] {'yh','yl','xh','z..., dimensions={0} | all-to-all | bytes 1310720 | tf_op jit(solution)/shard_map/all_to_all | solution.py:196
  47.2 0.0 copy-start
  47.2 0.0 copy-start.1
  47.2 0.0 copy-start.2
  47.2 4.5 %collective-permute-start = (bf16[256,5,2,128]{3,2,1,0:T(2,128)(2,1)S(1)}, bf16[256,5,2,128]{3,2,1,0:T(2,128)(2,1)S(1)}, u32[]{:S(2)}, u32[]{:S(2)}) collective-permute-start(bf16[256,5,2,128]{3,2,1,0:T(2,128)(2,1)S(1)} %all_to_all.10), channel_id=1, source_target_pairs={{0,1},{1,0},{2,3},{3,2},{4,5},{5,4},{6,7},{7,6},{8,9},{9,8},{10,11... | collective-permute-start | bytes 1966088 | tf_op jit(solution)/shard_map/ppermute | solution.py:198
  51.7 0.4 fusion
  52.1 0.1 reshape.20.names
  52.2 1.2 %collective-permute-done = bf16[256,5,2,128]{3,2,1,0:T(2,128)(2,1)S(1)} collective-permute-done((bf16[256,5,2,128]{3,2,1,0:T(2,128)(2,1)S(1)}, bf16[256,5,2,128]{3,2,1,0:T(2,128)(2,1)S(1)}, u32[]{:S(2)}, u32[]{:S(2)}) %collective-permute-start) | collective-permute-done | bytes 655392 | tf_op jit(solution)/shard_map/ppermute | solution.py:198
  53.4 1.4 %pick.1 = (bf16[16,256,128]{2,1,0:T(8,128)(2,1)S(1)}, f32[8,128]{1,0:T(8,128)S(1)}) custom-call(s32[1024]{0:T(1024)S(1)} %reshape.20.names, bf16[16,16,5,2,128]{4,3,2,1,0:T(2,128)(2,1)S(1)} %bitcast.3, bf16[16,16,5,2,128]{4,3,2,1,0:T(2,128)(2,1)S(1)} %bitcast.4), custom_call_target="tpu_custom_call" | custom-call | tf_op jit(solution)/shard_map/pick/pallas_call | solution.py:201
  54.8 20.1 %all_to_all.11.picked = bf16[16,256,128]{2,1,0:T(8,128)(2,1)S(1)} all-to-all(bf16[16,256,128]{2,1,0:T(8,128)(2,1)S(1)} %get-tuple-element.4), channel_id=1, replica_groups=mesh['yh'=4,'yl'=2,'xh'=2,'zh'=4,'zl'=2,'xl'=2,'c'=2] {'yl','xh','zl','xl'}, dimensions={0} | all-to-all | bytes 2097152 | tf_op jit(solution)/shard_map/all_to_all | solution.py:212
  75.0 0.0 copy-done
  75.0 0.0 copy-done.1
  75.0 0.0 copy-done.2
  75.0 5.1 %product.1 = (bf16[1,1024,1024]{2,1,0:T(8,128)(2,1)}, f32[1,1024]{1,0:T(1,128)}) custom-call(s32[1,4]{1,0:T(1,128)S(1)} %copy-done.2, bf16[16,256,128]{2,1,0:T(8,128)(2,1)S(1)} %all_to_all.11.picked, f32[8,128]{1,0:T(8,128)S(1)} %get-tuple-element.5.far, bf16[1,1024,1024]{2,1,0:T(8,128)(2,1)S(1)} %copy-done, f32[1,1024]{1,0:T(1,128)S(1)} %copy-done.1), custom_call_target="tpu_custom_call" | custom-call | tf_op jit(solution)/shard_map/product/pallas_call | solution.py:214
Async XLA Ops:
  47.2 27.8 %copy-start = (bf16[1,1024,1024]{2,1,0:T(8,128)(2,1)S(1)}, bf16[1,1024,1024]{2,1,0:T(8,128)(2,1)}, u32[]{:S(2)}) copy-start(bf16[1,1024,1024]{2,1,0:T(8,128)(2,1)} %factor.1) | copy-start | bytes 6291460
  47.2 27.8 %copy-start.1 = (f32[1,1024]{1,0:T(1,128)S(1)}, f32[1,1024]{1,0:T(1,128)}, u32[]{:S(2)}) copy-start(f32[1,1024]{1,0:T(1,128)} %diag.1) | copy-start | bytes 12292
  47.2 27.8 %copy-start.2 = (s32[1,4]{1,0:T(1,128)S(1)}, s32[1,4]{1,0:T(1,128)}, u32[]{:S(2)}) copy-start(s32[1,4]{1,0:T(1,128)} %structure.1) | copy-start | bytes 52
  47.2 6.2 %collective-permute-start = (bf16[256,5,2,128]{3,2,1,0:T(2,128)(2,1)S(1)}, bf16[256,5,2,128]{3,2,1,0:T(2,128)(2,1)S(1)}, u32[]{:S(2)}, u32[]{:S(2)}) collective-permute-start(bf16[256,5,2,128]{3,2,1,0:T(2,128)(2,1)S(1)} %all_to_all.10), channel_id=1, source_target_pairs={{0,1},{1,0},{2,3},{3,2},{4,5},{5,4},{6,7},{7,6},{8,9},{9,8},{10,11... | collective-permute-start | bytes 1966088 | tf_op jit(solution)/shard_map/ppermute | solution.py:198

commit v7 on v5

--- a/solution.py
+++ b/solution.py
@@ -7,8 +7,8 @@
 
 SIZES = dict(yh=4, yl=2, xh=2, zh=4, zl=2, xl=2, c=2)
 AXES = tuple(SIZES)
-CHIPS = AXES[:-1]
-NEAR = ("yl", "xh", "zl", "xl")
+NEAR = ("yl", "zl", "xh", "xl")
+CHIPS = ("yh", "zh") + NEAR
 NB = 16
 NU = 16
 S = 4
@@ -30,7 +30,13 @@
 
 def place():
     yh, yl, xh, zh, zl, xl, core = (lax.axis_index(a) for a in AXES)
-    return 4 * yh + 2 * yl + xh, 4 * zh + 2 * zl + xl, core
+    near = 8 * yl + 4 * zl + 2 * xh + xl
+    return 4 * yh + 2 * yl + xh, 4 * zh + 2 * zl + xl, core, 4 * yh + zh, near
+
+
+def shares(n):
+    high, middle, low = n >> 2, (n >> 1) & 1, n & 1
+    return 64 * high + 8 * middle + 2 * low, 16 * high + 4 * middle + low
 
 
 def deal_kernel(structure_hbm, sigma_hbm, dealt, structure, sigma, out, sems, out_sems):
@@ -42,13 +48,14 @@
         copy.start()
     for copy in copies:
         copy.wait()
-    r, b, core = place()
+    r, b, core, _, _ = place()
     lane, row = iota((8, 128), 1), iota((8, 128), 0)
     extra = jnp.zeros((8, 128), jnp.float32)
     for k in range(S):
-        extra = jnp.where(lane == k, structure[0, k].astype(jnp.float32), extra)
+        for h, share in enumerate(shares(structure[0, k])):
+            extra = jnp.where(lane == S * h + k, share.astype(jnp.float32), extra)
     start = pl.multiple_of(128 * core, 128)
-    square = sigma[pl.ds(start, 128), :].astype(jnp.float32)
+    square = -sigma[pl.ds(start, 128), :].astype(jnp.float32)
     far = jnp.where(apart((128, 128)) == 64, square, 0.0)
     extra = jnp.where(row == 1, jnp.sum(far, axis=0, keepdims=True), extra)
     extra = extra[:2].astype(jnp.bfloat16)
@@ -57,15 +64,15 @@
         low = jnp.where(r == b, (u // 8 > core).astype(jnp.int32), (r > b).astype(jnp.int32))
         tiles = []
         for v in (2 * u, 2 * u + 1):
-            tile = sigma[pl.ds(8 * v, 8), :].astype(jnp.float32)
+            tile = -sigma[pl.ds(8 * v, 8), :].astype(jnp.float32)
             keep = kept(lane - row - 8 * v, low)
             tiles.append(jnp.where(keep, tile, pltpu.roll(tile, 64, 1)))
         tile = jnp.where(first, *tiles)
         for j in range(4):
-            out[u // 4, u % 4, j] = tile[2 * j : 2 * j + 2].astype(jnp.bfloat16)
-        out[u // 4, u % 4, 4] = extra
+            out[u, j] = tile[2 * j : 2 * j + 2].astype(jnp.bfloat16)
+        out[u, 4] = extra
     spread = [
-        pltpu.make_async_copy(out, dealt.at[yh, :, zh], out_sems.at[yh, zh])
+        pltpu.make_async_copy(out, dealt.at[yh, zh], out_sems.at[yh, zh])
         for yh in range(4)
         for zh in range(4)
     ]
@@ -76,30 +83,31 @@
 
 
 def pick_kernel(names, own, other, out, far):
-    r_me, b_me, core = place()
-    y0, z0 = r_me // 4 * 4, b_me // 4 * 4
+    _, _, core, box, near = place()
     west = iota((8, 128), 1) < 64
 
     def run(left, right):
-        mine = (r_me * NB + b_me) * S
+        mine = (box * NU + near) * 2 * S
         for k in range(S):
-            at = names[mine + k]
+            at = names[mine + k] + names[mine + S + k]
             for g, half in enumerate((left, right)):
-                far[4 * g + k : 4 * g + k + 1, :] = half[at, at, 4].astype(jnp.float32)[1:2]
-
-        def step(t, carry):
-            first = ((y0 + t // 4) * NB + z0 + t % 4) * S
-            name = [names[first + k] for k in range(S)]
-            for q, (k, l) in enumerate(ORDER):
-                at = (name[k], name[l], pl.ds(0, 4))
-                one = left[at].astype(jnp.float32).reshape(8, 128)
-                two = right[at].astype(jnp.float32).reshape(8, 128)
-                both = [jnp.where(west, one, two), jnp.where(west, two, one)]
-                rows = pl.ds(16 * q, 16)
-                out[t, rows, :] = jnp.concatenate(both, axis=0).astype(jnp.bfloat16)
+                far[4 * g + k : 4 * g + k + 1, :] = half[at, 4].astype(jnp.float32)[1:2]
+
+        def step(i, carry):
+            for t in range(4):
+                t = 4 * i + t
+                first = (box * NU + t) * 2 * S
+                name = [names[first + k] for k in range(2 * S)]
+                for q, (k, l) in enumerate(ORDER):
+                    at = (name[k] + name[S + l], pl.ds(0, 4))
+                    one = left[at].astype(jnp.float32).reshape(8, 128)
+                    two = right[at].astype(jnp.float32).reshape(8, 128)
+                    both = [jnp.where(west, one, two), jnp.where(west, two, one)]
+                    rows = pl.ds(16 * q, 16)
+                    out[t, rows, :] = jnp.concatenate(both, axis=0).astype(jnp.bfloat16)
             return carry
 
-        lax.fori_loop(0, NU, step, 0)
+        lax.fori_loop(0, NU // 4, step, 0)
 
     @pl.when(core == 0)
     def _():
@@ -147,12 +155,12 @@
                     gram[down, across] = value
                     if l > k:
                         gram[across, down] = value.T
-        minus = jnp.dot(gram[rows, :], factor[0], preferred_element_type=jnp.float32)
-        staged[k] = (-minus).astype(jnp.bfloat16)
+        product = jnp.dot(gram[rows, :], factor[0], preferred_element_type=jnp.float32)
+        staged[k] = product.astype(jnp.bfloat16)
         copies.append(pltpu.make_async_copy(staged.at[k], off.at[0, rows], sems.at[k]))
         copies[k].start()
-        total += jnp.sum(
-            factor[0, rows, :].astype(jnp.float32) * minus, axis=0, keepdims=True
+        total -= jnp.sum(
+            factor[0, rows, :].astype(jnp.float32) * product, axis=0, keepdims=True
         )
     variance[...] = total
     for copy in copies:
@@ -168,13 +176,13 @@
     message = (5, 2, 128)
     dealt = pl.pallas_call(
         deal_kernel,
-        out_shape=jax.ShapeDtypeStruct((4, 4, 4, 4) + message, jnp.bfloat16),
+        out_shape=jax.ShapeDtypeStruct((4, 4, NU) + message, jnp.bfloat16),
         in_specs=[anywhere, anywhere],
         out_specs=anywhere,
         scratch_shapes=[
             smem(structure.shape, jnp.int32),
             vmem(sigma.shape, jnp.bfloat16),
-            vmem((4, 4) + message, jnp.bfloat16),
+            vmem((NU,) + message, jnp.bfloat16),
             pltpu.SemaphoreType.DMA((2,)),
             pltpu.SemaphoreType.DMA((4, 4)),
         ],
@@ -183,8 +191,7 @@
     own = lax.all_to_all(dealt.reshape((NB * NB,) + message), CHIPS, 0, 0, tiled=True)
     flip = [(d, d ^ 1) for d in range(2 * NB * NB)]
     other = lax.ppermute(own, AXES, flip)
-    grid = (NB, NB) + message
-    names = own[:, 4, 0, :S].astype(jnp.int32).reshape(NB * NB * S)
+    names = own[:, 4, 0, : 2 * S].astype(jnp.int32).reshape(NB * NB * 2 * S)
     chosen, far = pl.pallas_call(
         pick_kernel,
         out_shape=(
@@ -195,7 +202,7 @@
         out_specs=(whole, whole),
         compiler_params=pltpu.CompilerParams(vmem_limit_bytes=6 << 20),
         name="pick",
-    )(names, own.reshape(grid), other.reshape(grid))
+    )(names, own, other)
     picked = lax.all_to_all(chosen, NEAR, 0, 0, tiled=True)
 
     off, variance = pl.pallas_call(

time: 80.6 us -> 80 us (level)
  blocking collectives: 64.8 us -> 63.8 us
    all_to_all x1, blocking collectives: 20.1 us -> 18.8 us  [body(): picked = lax.all_to_all(chosen, NEAR, 0, 0, tiled=True)]
where the time goes in v7:
time: 80 us; the launch traced here: 79.7 us
  blocking collectives  63.8 us (80%)
  Pallas kernels  8.39 us (10%)
  starting transfers between devices  5.2 us (6%)
  waiting for transfers between devices  1.17 us (1%)
    all_to_all x1, blocking collectives, body(): lax.all_to_all(dealt.reshape((NB * NB,) + message), CHIPS, 0, 0, tiled=True)  44.9 us
    all_to_all x1, blocking collectives, body(): picked = lax.all_to_all(chosen, NEAR, 0, 0, tiled=True)  18.8 us
    ppermute x1, starting transfers between devices, body(): other = lax.ppermute(own, AXES, flip)  5.2 us
    pallas_call x1, Pallas kernels, body(): pl.pallas_call(product_kernel, out_shape=(jax.ShapeDtypeStruct(factor.sha...  4.99 us
    pallas_call x1, Pallas kernels, body(): pl.pallas_call(deal_kernel, out_shape=jax.ShapeDtypeStruct((4, 4, NU) + m...  1.93 us
  transfers between devices with their start and end apart: 1, of which 1 were waited for; matrix products, arithmetic and copies ran while one was open for 1% of the time, Pallas kernels for 0%

profile of v7, /device:TPU:1, one launch (start us, length us, event | category | flops | bytes accessed | tf_op | source)
XLA Modules:
  0.0 79.7 jit_solution(11683887169395008024)
XLA Ops:
  0.6 1.9 %deal.1 = bf16[4,4,16,5,2,128]{5,4,3,2,1,0:T(2,128)(2,1)} custom-call(s32[1,4]{1,0:T(1,128)} %structure.1, bf16[256,128]{1,0:T(8,128)(2,1)} %sigma_hbm.1), custom_call_target="tpu_custom_call" | custom-call | tf_op jit(solution)/shard_map/deal/pallas_call | solution.py:177
  2.6 44.9 %all_to_all.10.own = bf16[256,5,2,128]{3,2,1,0:T(2,128)(2,1)S(1)} all-to-all(bf16[256,5,2,128]{3,2,1,0:T(2,128)(2,1)} %bitcast.1), channel_id=1, replica_groups=mesh['yh'=4,'yl'=2,'xh'=2,'zh'=4,'zl'=2,'xl'=2,'c'=2] {'yh','zh','yl','z..., dimensions={0} | all-to-all | bytes 1310720 | tf_op jit(solution)/shard_map/all_to_all | solution.py:191
  47.5 0.0 copy-start
  47.5 0.0 copy-start.1
  47.5 0.0 copy-start.2
  47.5 5.2 %collective-permute-start = (bf16[256,5,2,128]{3,2,1,0:T(2,128)(2,1)S(1)}, bf16[256,5,2,128]{3,2,1,0:T(2,128)(2,1)S(1)}, u32[]{:S(2)}, u32[]{:S(2)}) collective-permute-start(bf16[256,5,2,128]{3,2,1,0:T(2,128)(2,1)S(1)} %all_to_all.10.own), channel_id=1, source_target_pairs={{0,1},{1,0},{2,3},{3,2},{4,5},{5,4},{6,7},{7,6},{8,9},{9,8},{10,11... | collective-permute-start | bytes 1966088 | tf_op jit(solution)/shard_map/ppermute | solution.py:193
  52.7 0.4 fusion
  53.1 0.1 reshape.12.names
  53.2 1.2 %collective-permute-done.other = bf16[256,5,2,128]{3,2,1,0:T(2,128)(2,1)S(1)} collective-permute-done((bf16[256,5,2,128]{3,2,1,0:T(2,128)(2,1)S(1)}, bf16[256,5,2,128]{3,2,1,0:T(2,128)(2,1)S(1)}, u32[]{:S(2)}, u32[]{:S(2)}) %collective-permute-start) | collective-permute-done | bytes 655392 | tf_op jit(solution)/shard_map/ppermute | solution.py:193
  54.4 1.5 %pick.1 = (bf16[16,256,128]{2,1,0:T(8,128)(2,1)S(1)}, f32[8,128]{1,0:T(8,128)S(1)}) custom-call(s32[2048]{0:T(1024)S(1)} %reshape.12.names, bf16[256,5,2,128]{3,2,1,0:T(2,128)(2,1)S(1)} %all_to_all.10.own, bf16[256,5,2,128]{3,2,1,0:T(2,128)(2,1)S(1)} %collective-permute-done.other), custom_call_target="tpu_custom_call" | custom-call | tf_op jit(solution)/shard_map/pick/pallas_call | solution.py:195
  55.9 18.8 %all_to_all.11.picked = bf16[16,256,128]{2,1,0:T(8,128)(2,1)S(1)} all-to-all(bf16[16,256,128]{2,1,0:T(8,128)(2,1)S(1)} %get-tuple-element.4), channel_id=1, replica_groups=mesh['yh'=4,'yl'=2,'xh'=2,'zh'=4,'zl'=2,'xl'=2,'c'=2] {'yl','zl','xh','xl'}, dimensions={0} | all-to-all | bytes 2097152 | tf_op jit(solution)/shard_map/all_to_all | solution.py:206
  74.7 0.0 copy-done
  74.7 0.0 copy-done.1
  74.7 0.0 copy-done.2
  74.7 5.0 %product.1 = (bf16[1,1024,1024]{2,1,0:T(8,128)(2,1)}, f32[1,1024]{1,0:T(1,128)}) custom-call(s32[1,4]{1,0:T(1,128)S(1)} %copy-done.2, bf16[16,256,128]{2,1,0:T(8,128)(2,1)S(1)} %all_to_all.11.picked, f32[8,128]{1,0:T(8,128)S(1)} %get-tuple-element.5.far, bf16[1,1024,1024]{2,1,0:T(8,128)(2,1)S(1)} %copy-done, f32[1,1024]{1,0:T(1,128)S(1)} %copy-done.1), custom_call_target="tpu_custom_call" | custom-call | tf_op jit(solution)/shard_map/product/pallas_call | solution.py:208
Async XLA Ops:
  47.5 27.2 %copy-start = (bf16[1,1024,1024]{2,1,0:T(8,128)(2,1)S(1)}, bf16[1,1024,1024]{2,1,0:T(8,128)(2,1)}, u32[]{:S(2)}) copy-start(bf16[1,1024,1024]{2,1,0:T(8,128)(2,1)} %factor.1) | copy-start | bytes 6291460
  47.5 27.2 %copy-start.1 = (f32[1,1024]{1,0:T(1,128)S(1)}, f32[1,1024]{1,0:T(1,128)}, u32[]{:S(2)}) copy-start(f32[1,1024]{1,0:T(1,128)} %diag.1) | copy-start | bytes 12292
  47.5 27.2 %copy-start.2 = (s32[1,4]{1,0:T(1,128)S(1)}, s32[1,4]{1,0:T(1,128)}, u32[]{:S(2)}) copy-start(s32[1,4]{1,0:T(1,128)} %structure.1) | copy-start | bytes 52
  47.5 6.9 %collective-permute-start = (bf16[256,5,2,128]{3,2,1,0:T(2,128)(2,1)S(1)}, bf16[256,5,2,128]{3,2,1,0:T(2,128)(2,1)S(1)}, u32[]{:S(2)}, u32[]{:S(2)}) collective-permute-start(bf16[256,5,2,128]{3,2,1,0:T(2,128)(2,1)S(1)} %all_to_all.10.own), channel_id=1, source_target_pairs={{0,1},{1,0},{2,3},{3,2},{4,5},{5,4},{6,7},{7,6},{8,9},{9,8},{10,11... | collective-permute-start | bytes 1966088 | tf_op jit(solution)/shard_map/ppermute | solution.py:193

commit v8 on v7

--- a/solution.py
+++ b/solution.py
@@ -155,10 +155,15 @@
                     gram[down, across] = value
                     if l > k:
                         gram[across, down] = value.T
+        if k % 2 == 0:
+            continue
+        half, rows = k // 2, pl.ds(512 * (k // 2), 512)
         product = jnp.dot(gram[rows, :], factor[0], preferred_element_type=jnp.float32)
-        staged[k] = product.astype(jnp.bfloat16)
-        copies.append(pltpu.make_async_copy(staged.at[k], off.at[0, rows], sems.at[k]))
-        copies[k].start()
+        staged[half] = product.astype(jnp.bfloat16)
+        copies.append(
+            pltpu.make_async_copy(staged.at[half], off.at[0, rows], sems.at[half])
+        )
+        copies[half].start()
         total -= jnp.sum(
             factor[0, rows, :].astype(jnp.float32) * product, axis=0, keepdims=True
         )
@@ -215,8 +220,8 @@
         out_specs=(anywhere, whole),
         scratch_shapes=[
             vmem((1024, 1024), jnp.bfloat16),
-            vmem((S, 256, 1024), jnp.bfloat16),
-            pltpu.SemaphoreType.DMA((S,)),
+            vmem((2, 512, 1024), jnp.bfloat16),
+            pltpu.SemaphoreType.DMA((2,)),
         ],
         compiler_params=pltpu.CompilerParams(vmem_limit_bytes=24 << 20),
         name="product",

time: 80 us -> 80.4 us (level)
  no operation moved by 1% of the time
where the time goes in v8:
time: 80.4 us; the launch traced here: 80.1 us
  blocking collectives  63.8 us (79%)
  Pallas kernels  8.78 us (11%)
  starting transfers between devices  5.2 us (6%)
  waiting for transfers between devices  1.17 us (1%)
    all_to_all x1, blocking collectives, body(): lax.all_to_all(dealt.reshape((NB * NB,) + message), CHIPS, 0, 0, tiled=True)  44.9 us
    all_to_all x1, blocking collectives, body(): picked = lax.all_to_all(chosen, NEAR, 0, 0, tiled=True)  18.8 us
    pallas_call x1, Pallas kernels, body(): pl.pallas_call(product_kernel, out_shape=(jax.ShapeDtypeStruct(factor.sha...  5.38 us
    ppermute x1, starting transfers between devices, body(): other = lax.ppermute(own, AXES, flip)  5.2 us
    pallas_call x1, Pallas kernels, body(): pl.pallas_call(deal_kernel, out_shape=jax.ShapeDtypeStruct((4, 4, NU) + m...  1.93 us
  transfers between devices with their start and end apart: 1, of which 1 were waited for; matrix products, arithmetic and copies ran while one was open for 1% of the time, Pallas kernels for 0%

profile of v8, /device:TPU:1, one launch (start us, length us, event | category | flops | bytes accessed | tf_op | source)
XLA Modules:
  0.0 80.1 jit_solution(17616162705062845770)
XLA Ops:
  0.6 1.9 %deal.1 = bf16[4,4,16,5,2,128]{5,4,3,2,1,0:T(2,128)(2,1)} custom-call(s32[1,4]{1,0:T(1,128)} %structure.1, bf16[256,128]{1,0:T(8,128)(2,1)} %sigma_hbm.1), custom_call_target="tpu_custom_call" | custom-call | tf_op jit(solution)/shard_map/deal/pallas_call | solution.py:182
  2.6 44.9 %all_to_all.10.own = bf16[256,5,2,128]{3,2,1,0:T(2,128)(2,1)S(1)} all-to-all(bf16[256,5,2,128]{3,2,1,0:T(2,128)(2,1)} %bitcast.1), channel_id=1, replica_groups=mesh['yh'=4,'yl'=2,'xh'=2,'zh'=4,'zl'=2,'xl'=2,'c'=2] {'yh','zh','yl','z..., dimensions={0} | all-to-all | bytes 1310720 | tf_op jit(solution)/shard_map/all_to_all | solution.py:196
  47.5 0.0 copy-start
  47.5 0.0 copy-start.1
  47.5 0.0 copy-start.2
  47.5 5.2 %collective-permute-start = (bf16[256,5,2,128]{3,2,1,0:T(2,128)(2,1)S(1)}, bf16[256,5,2,128]{3,2,1,0:T(2,128)(2,1)S(1)}, u32[]{:S(2)}, u32[]{:S(2)}) collective-permute-start(bf16[256,5,2,128]{3,2,1,0:T(2,128)(2,1)S(1)} %all_to_all.10.own), channel_id=1, source_target_pairs={{0,1},{1,0},{2,3},{3,2},{4,5},{5,4},{6,7},{7,6},{8,9},{9,8},{10,11... | collective-permute-start | bytes 1966088 | tf_op jit(solution)/shard_map/ppermute | solution.py:198
  52.7 0.4 fusion
  53.1 0.1 reshape.12.names
  53.2 1.2 %collective-permute-done.other = bf16[256,5,2,128]{3,2,1,0:T(2,128)(2,1)S(1)} collective-permute-done((bf16[256,5,2,128]{3,2,1,0:T(2,128)(2,1)S(1)}, bf16[256,5,2,128]{3,2,1,0:T(2,128)(2,1)S(1)}, u32[]{:S(2)}, u32[]{:S(2)}) %collective-permute-start) | collective-permute-done | bytes 655392 | tf_op jit(solution)/shard_map/ppermute | solution.py:198
  54.4 1.5 %pick.1 = (bf16[16,256,128]{2,1,0:T(8,128)(2,1)S(1)}, f32[8,128]{1,0:T(8,128)S(1)}) custom-call(s32[2048]{0:T(1024)S(1)} %reshape.12.names, bf16[256,5,2,128]{3,2,1,0:T(2,128)(2,1)S(1)} %all_to_all.10.own, bf16[256,5,2,128]{3,2,1,0:T(2,128)(2,1)S(1)} %collective-permute-done.other), custom_call_target="tpu_custom_call" | custom-call | tf_op jit(solution)/shard_map/pick/pallas_call | solution.py:200
  55.9 18.8 %all_to_all.11.picked = bf16[16,256,128]{2,1,0:T(8,128)(2,1)S(1)} all-to-all(bf16[16,256,128]{2,1,0:T(8,128)(2,1)S(1)} %get-tuple-element.4), channel_id=1, replica_groups=mesh['yh'=4,'yl'=2,'xh'=2,'zh'=4,'zl'=2,'xl'=2,'c'=2] {'yl','zl','xh','xl'}, dimensions={0} | all-to-all | bytes 2097152 | tf_op jit(solution)/shard_map/all_to_all | solution.py:211
  74.7 0.0 copy-done
  74.7 0.0 copy-done.1
  74.7 0.0 copy-done.2
  74.7 5.4 %product.1 = (bf16[1,1024,1024]{2,1,0:T(8,128)(2,1)}, f32[1,1024]{1,0:T(1,128)}) custom-call(s32[1,4]{1,0:T(1,128)S(1)} %copy-done.2, bf16[16,256,128]{2,1,0:T(8,128)(2,1)S(1)} %all_to_all.11.picked, f32[8,128]{1,0:T(8,128)S(1)} %get-tuple-element.5.far, bf16[1,1024,1024]{2,1,0:T(8,128)(2,1)S(1)} %copy-done, f32[1,1024]{1,0:T(1,128)S(1)} %copy-done.1), custom_call_target="tpu_custom_call" | custom-call | tf_op jit(solution)/shard_map/product/pallas_call | solution.py:213
Async XLA Ops:
  47.5 27.2 %copy-start = (bf16[1,1024,1024]{2,1,0:T(8,128)(2,1)S(1)}, bf16[1,1024,1024]{2,1,0:T(8,128)(2,1)}, u32[]{:S(2)}) copy-start(bf16[1,1024,1024]{2,1,0:T(8,128)(2,1)} %factor.1) | copy-start | bytes 6291460
  47.5 27.2 %copy-start.1 = (f32[1,1024]{1,0:T(1,128)S(1)}, f32[1,1024]{1,0:T(1,128)}, u32[]{:S(2)}) copy-start(f32[1,1024]{1,0:T(1,128)} %diag.1) | copy-start | bytes 12292
  47.5 27.2 %copy-start.2 = (s32[1,4]{1,0:T(1,128)S(1)}, s32[1,4]{1,0:T(1,128)}, u32[]{:S(2)}) copy-start(s32[1,4]{1,0:T(1,128)} %structure.1) | copy-start | bytes 52
  47.5 6.9 %collective-permute-start = (bf16[256,5,2,128]{3,2,1,0:T(2,128)(2,1)S(1)}, bf16[256,5,2,128]{3,2,1,0:T(2,128)(2,1)S(1)}, u32[]{:S(2)}, u32[]{:S(2)}) collective-permute-start(bf16[256,5,2,128]{3,2,1,0:T(2,128)(2,1)S(1)} %all_to_all.10.own), channel_id=1, source_target_pairs={{0,1},{1,0},{2,3},{3,2},{4,5},{5,4},{6,7},{7,6},{8,9},{9,8},{10,11... | collective-permute-start | bytes 1966088 | tf_op jit(solution)/shard_map/ppermute | solution.py:198
